TPU v7x, 32 devices: a whole 2x2x4 slice. The times are simulated.
32 devices in a mesh: subj: 2 (over x), ha: 8 (over z, y), dev: 2 (over core).
Axes of the slice: x: 2, y: 2, z: 4, core: 2. Of those that a mesh axis runs over, the one named last changes fastest.
Arguments:
- brain_image: float32 [64, 256, 768], P('subj', 'ha', 'dev'), parts along dimension 0, may hold values from -6 to 6
- adjoint_field: float32 [64, 256, 768], P('subj', 'ha', 'dev'), parts along dimension 0, may hold values from -6 to 6
- velocity_modes: float32 [6, 16, 32, 32], P('subj'), parts along dimension 0, may hold values from -4 to 4
Outputs:
- adjoint_end: float32 [64, 256, 768], P('subj', 'ha', 'dev'), parts along dimension 0
- image_end: float32 [64, 256, 768], P('subj', 'ha', 'dev'), parts along dimension 0
- velocity_next: float32 [6, 16, 32, 32], P('subj'), parts along dimension 0
There are 2 independent parts, one for each index of `subj`. A program takes and returns all parts, laid end to end along the dimension named above; each array names one. Nothing has to cross between parts.
All inputs are finite; a program needn't handle non-finite values.
Results may differ from a plain program's by a relative error of at most 0.0003.
Values sent between devices are 32-bit elements; how exact they have to be, the bound alone decides.
A program may use at most 128 MiB of HBM per device.

v0:
```python
import functools
import math

import jax
import jax.numpy as jnp
import ml_dtypes
import numpy as np
from jax import lax
from jax.experimental import pallas as pl
from jax.experimental.pallas import tpu as pltpu
from jax.sharding import PartitionSpec as P

STEPS = 4
HALO = 2 * STEPS
STEP_SIZE = 4.0
STIFFNESS = 2.0
LANES = 128
F32 = jnp.float32
BF16 = jnp.bfloat16


def wavenumbers(modes):
    column = np.arange(modes)
    return np.where(column <= modes // 2, column, column - modes // 2)


def basis(positions, length, modes):
    phase = positions[:, None] * wavenumbers(modes)[None, :] % length
    angles = phase * (2.0 * math.pi / length)
    cosine = np.arange(modes)[None, :] <= modes // 2
    table = np.where(cosine, np.cos(angles), np.sin(angles))
    inside = (positions >= 0) & (positions < length)
    return np.where(inside[:, None], table, 0.0).astype(np.float32)


def halves(table):
    high = table.astype(ml_dtypes.bfloat16)
    low = (table - high.astype(np.float32)).astype(ml_dtypes.bfloat16)
    return high, low


def wrapped(start, rows, total, length):
    gap = np.full(total - rows - 2 * HALO, -1)
    after = np.arange(start + rows, start + rows + HALO)
    before = np.arange(start - HALO, start)
    return np.concatenate([np.arange(start, start + rows), after, gap, before])


def mode_factor(lengths, modes):
    eigen, weight = [], []
    for length, count in zip(lengths, modes):
        eigen.append(2.0 - 2.0 * np.cos(wavenumbers(count) * (2.0 * math.pi / length)))
        weight.append(np.where(np.arange(count) == 0, length, length / 2.0))
    value = eigen[0][:, None, None] + eigen[1][None, :, None] + eigen[2][None, None, :]
    norm = weight[0][:, None, None] * weight[1][None, :, None] * weight[2][None, None, :]
    return STEP_SIZE * math.sqrt(math.prod(modes)) / (norm * (1.0 + STIFFNESS * value) ** 2)


def split(value):
    high = value.astype(BF16)
    return high, (value - high.astype(F32)).astype(BF16)


def expand_kernel(planes, modes_x, modes, v_ref, bx_ref, by_ref, bz_ref, coefs):
    height, depth = coefs[0].shape[1:]
    group = lax.broadcasted_iota(jnp.int32, (height, LANES), 1) // modes

    def body(x, carry):
        weighted = bx_ref[x, 0] * v_ref[0]
        for a in range(1, modes_x):
            weighted = weighted + bx_ref[x, a] * v_ref[a]
        high, low = split(weighted)
        rows = jnp.concatenate([high, low, high], axis=0)
        mixed = jnp.dot(by_ref[...], rows, preferred_element_type=F32)
        top = mixed.astype(BF16).astype(F32)
        rest = mixed - top
        total = jnp.ones((height, depth), F32)
        for c in range(3):
            first = pltpu.roll(top, (-c * modes) % LANES, 1) if c else top
            second = pltpu.roll(top, ((1 - c) * modes) % LANES, 1) if c != 1 else top
            third = pltpu.roll(rest, ((2 - c) * modes) % LANES, 1) if c != 2 else rest
            left = jnp.where(group == 0, first, jnp.where(group == 1, second, third))
            speed = jnp.dot(left.astype(BF16), bz_ref[...], preferred_element_type=F32)
            plus = jnp.maximum(speed, 0.0)
            minus = jnp.maximum(-speed, 0.0)
            coefs[1 + 2 * c][x] = plus
            coefs[2 + 2 * c][x] = minus
            total = total - (plus + minus)
        coefs[0][x] = total
        return carry

    lax.fori_loop(0, planes, body, 0)


def gather_field(q_ref, yh_ref, zt_ref, field):
    planes, rows, depth = q_ref.shape
    height = field.shape[1]
    field[0] = jnp.zeros(field.shape[1:], F32)
    field[planes + 1] = jnp.zeros(field.shape[1:], F32)

    def body(x, carry):
        field[x + 1, 0:rows, 0:depth] = q_ref[x]
        field[x + 1, rows:height, 0:depth] = yh_ref[x]
        field[x + 1, :, depth : depth + LANES] = zt_ref[x]
        return carry

    lax.fori_loop(0, planes, body, 0)


def stencil(src, x, coefs, rows, depth):
    height, width = src.shape[1:]
    strips = height // 8
    wanted = rows // 8
    row = lax.broadcasted_iota(jnp.int32, (8, depth), 0)
    tiles = {}
    ups = {}
    downs = {}

    def tile(t):
        t = t % strips
        if t not in tiles:
            tiles[t] = src[x + 1, 8 * t : 8 * t + 8, :]
        return tiles[t]

    def up(t):
        t = t % strips
        if t not in ups:
            ups[t] = pltpu.roll(tile(t)[:, :depth], 1, 0)
        return ups[t]

    def down(t):
        t = t % strips
        if t not in downs:
            downs[t] = pltpu.roll(tile(t)[:, :depth], 7, 0)
        return downs[t]

    results = []
    for t in range(wanted):
        part = pl.ds(8 * t, 8)

        def coef(index):
            return coefs[index][x, part, 0:depth]

        q = tile(t)
        total = coef(0) * q[:, :depth]
        total = total + coef(1) * src[x, part, 0:depth] + coef(2) * src[x + 2, part, 0:depth]
        total = total + coef(3) * jnp.where(row == 0, up(t - 1), up(t))
        total = total + coef(4) * jnp.where(row == 7, down(t + 1), down(t))
        total = total + coef(5) * pltpu.roll(q, 1, 1)[:, :depth]
        total = total + coef(6) * pltpu.roll(q, width - 1, 1)[:, :depth]
        results.append(total)
    return results


def transport_kernel(
    planes, modes_x, modes, v_ref, bx_ref, by_ref, bz_ref, q_ref, yh_ref, zt_ref, out_ref, *scratch
):
    field, middle = scratch[:2]
    coefs = scratch[2:]
    height, width = field.shape[1:]
    rows, depth = q_ref.shape[1:]
    gather_field(q_ref, yh_ref, zt_ref, field)
    middle[0] = jnp.zeros((height, width), F32)
    middle[planes + 1] = jnp.zeros((height, width), F32)
    expand_kernel(planes, modes_x, modes, v_ref, bx_ref, by_ref, bz_ref, coefs)

    def first(x, carry):
        for t, value in enumerate(stencil(field, x, coefs, height, width)):
            middle[x + 1, 8 * t : 8 * t + 8, :] = value
        return carry

    def second(x, carry):
        for t, value in enumerate(stencil(middle, x, coefs, height, width)):
            part = pl.ds(8 * t, 8)
            field[x + 1, part, :] = 0.5 * (field[x + 1, part, :] + value)
        return carry

    def last(x, carry):
        for t, value in enumerate(stencil(middle, x, coefs, rows, depth)):
            part = pl.ds(8 * t, 8)
            out_ref[x, part, :] = 0.5 * (field[x + 1, part, 0:depth] + value)
        return carry

    def step(i, carry):
        lax.fori_loop(0, planes, first, 0)
        lax.fori_loop(0, planes, second, 0)
        return carry

    lax.fori_loop(0, STEPS - 1, step, 0)
    lax.fori_loop(0, planes, first, 0)
    lax.fori_loop(0, planes, last, 0)


def project_kernel(
    planes, modes_x, adj_ref, q_ref, yh_ref, zt_ref, bx_ref, by_ref, bz_ref, out_ref, field, forcing, inner
):
    height, width = field.shape[1:]
    rows, depth = q_ref.shape[1:]
    gather_field(q_ref, yh_ref, zt_ref, field)

    def body(x, carry):
        plane = field[x + 1]
        half = 0.5 * adj_ref[x]
        slopes = (
            field[x + 2, 0:rows, 0:depth] - field[x, 0:rows, 0:depth],
            (pltpu.roll(plane, height - 1, 0) - pltpu.roll(plane, 1, 0))[0:rows, 0:depth],
            (pltpu.roll(plane, width - 1, 1) - pltpu.roll(plane, 1, 1))[0:rows, 0:depth],
        )
        for c in range(3):
            high, low = split(half * slopes[c])
            columns = slice(c * depth, (c + 1) * depth)
            forcing[pl.ds(x * 2 * rows, rows), columns] = high
            forcing[pl.ds(x * 2 * rows + rows, rows), columns] = low
        return carry

    lax.fori_loop(0, planes, body, 0)
    chunk = 8

    def multiply(i, carry):
        start = i * (chunk * 2 * rows)
        wide = jnp.dot(
            forcing[pl.ds(start, chunk * 2 * rows), :], bz_ref[...], preferred_element_type=F32
        )
        wide = wide[:, 0:LANES] + wide[:, LANES : 2 * LANES]
        wide = wide.reshape(chunk, 2 * rows, LANES)
        inner[pl.ds(i * chunk, chunk)] = wide[:, 0:rows] + wide[:, rows : 2 * rows]
        return carry

    lax.fori_loop(0, planes // chunk, multiply, 0)

    def finish(a, carry):
        total = bx_ref[0, a] * inner[0]
        for x in range(1, planes):
            total = total + bx_ref[x, a] * inner[x]
        high, low = split(total)
        stacked = jnp.concatenate([high, low, high], axis=0)
        out_ref[a] = jnp.dot(by_ref[...], stacked, preferred_element_type=F32)
        return carry

    lax.fori_loop(0, modes_x, finish, 0)


VMEM = pl.BlockSpec(memory_space=pltpu.VMEM)
SMEM = pl.BlockSpec(memory_space=pltpu.SMEM)
PARAMS = pltpu.CompilerParams(vmem_limit_bytes=60 * 1024 * 1024)


def halo_of(field):
    count = lax.axis_size("ha")
    forward = [(i, i + 1) for i in range(count - 1)]
    backward = [(i + 1, i) for i in range(count - 1)]
    before = lax.ppermute(field[:, -HALO:, :], "ha", forward)
    after = lax.ppermute(field[:, :HALO, :], "ha", backward)
    sides = lax.axis_size("dev")
    forward = [(i, i + 1) for i in range(sides - 1)]
    backward = [(i + 1, i) for i in range(sides - 1)]
    rows = jnp.concatenate([after, before], axis=1)
    head = jnp.concatenate([field[:, :, :HALO], rows[:, :, :HALO]], axis=1)
    tail = jnp.concatenate([field[:, :, -HALO:], rows[:, :, -HALO:]], axis=1)
    left = lax.ppermute(tail, "dev", forward)
    right = lax.ppermute(head, "dev", backward)
    gap = jnp.zeros(left.shape[:2] + (LANES - 2 * HALO,), F32)
    return rows, jnp.concatenate([right, gap, left], axis=2)


def per_device(brain_image, adjoint_field, velocity_modes):
    planes, rows, cols = brain_image.shape
    count_y = lax.axis_size("ha")
    count_z = lax.axis_size("dev")
    height, depth = rows * count_y, cols * count_z
    modes_x, modes = velocity_modes.shape[1:3]
    tall, wide = rows + 2 * HALO, cols + LANES
    index_y, index_z = lax.axis_index("ha"), lax.axis_index("dev")

    expand_y, expand_z, project_y, project_z = [], [], [], []
    for i in range(count_y):
        high, low = halves(basis(wrapped(i * rows, rows, tall, height), height, modes))
        expand_y.append(np.concatenate([high, high, low], axis=1))
        high, low = high[:rows].T, low[:rows].T
        project_y.append(np.concatenate([high, high, low], axis=1))
    for i in range(count_z):
        high, low = halves(basis(wrapped(i * cols, cols, wide, depth), depth, modes))
        high, low = high.T, low.T
        table = np.zeros((LANES, wide), ml_dtypes.bfloat16)
        table[: 3 * modes] = np.concatenate([high, low, high], axis=0)
        expand_z.append(table)
        table = np.zeros((3, cols, 2, LANES), ml_dtypes.bfloat16)
        for c in range(3):
            table[c, :, 0, c * modes : (c + 1) * modes] = high.T[:cols]
            table[c, :, 1, c * modes : (c + 1) * modes] = low.T[:cols]
        project_z.append(table.reshape(3 * cols, 2 * LANES))

    def pick(tables, index):
        return lax.dynamic_index_in_dim(jnp.asarray(np.stack(tables)), index, 0, keepdims=False)

    by_wide, by_back = pick(expand_y, index_y), pick(project_y, index_y)
    bz_wide, bz_back = pick(expand_z, index_z), pick(project_z, index_z)
    bx = jnp.asarray(basis(np.arange(planes), planes, modes_x))
    factor = mode_factor((planes, height, depth), (modes_x, modes, modes))
    factor = np.tile(factor, (1, 1, 3)).astype(np.float32)
    scale = 1.0 / math.sqrt(modes_x * modes * modes)

    def widen(value):
        return jnp.pad(value, ((0, 0), (0, 0), (0, LANES - 3 * modes)))

    plane = pltpu.VMEM((planes + 2, tall, wide), F32)
    transport = pl.pallas_call(
        functools.partial(transport_kernel, planes, modes_x, modes),
        out_shape=jax.ShapeDtypeStruct((planes, rows, cols), F32),
        in_specs=[VMEM, SMEM, VMEM, VMEM, VMEM, VMEM, VMEM],
        out_specs=VMEM,
        scratch_shapes=[plane, plane] + [pltpu.VMEM((planes, tall, wide), F32)] * 7,
        compiler_params=PARAMS,
        cost_estimate=pl.CostEstimate(
            flops=200 * planes * tall * wide, bytes_accessed=60_000_000, transcendentals=0
        ),
        name="transport",
    )
    project = pl.pallas_call(
        functools.partial(project_kernel, planes, modes_x),
        out_shape=jax.ShapeDtypeStruct((modes_x, modes, LANES), F32),
        in_specs=[VMEM, VMEM, VMEM, VMEM, SMEM, VMEM, VMEM],
        out_specs=VMEM,
        scratch_shapes=[
            plane,
            pltpu.VMEM((planes * 2 * rows, 3 * cols), BF16),
            pltpu.VMEM((planes, rows, LANES), F32),
        ],
        compiler_params=PARAMS,
        name="project",
    )

    old = velocity_modes.transpose(1, 2, 0, 3).reshape(modes_x, modes, 3 * modes)
    adjoint_halo = halo_of(adjoint_field)
    image_halo = halo_of(brain_image)
    adjoint_end = transport(
        widen(old * -scale), bx, by_wide, bz_wide, adjoint_field, *adjoint_halo
    )
    partial = project(adjoint_end, brain_image, *image_halo, bx, by_back, bz_back)
    summed = lax.psum(partial[:, :, : 3 * modes], ("ha", "dev"))
    updated = old + factor * summed
    image_end = transport(widen(updated * scale), bx, by_wide, bz_wide, brain_image, *image_halo)
    velocity_next = updated.reshape(modes_x, modes, 3, modes).transpose(2, 0, 1, 3)
    return (adjoint_end, image_end, velocity_next)


def solution(mesh):
    placed = (P("subj", "ha", "dev"), P("subj", "ha", "dev"), P("subj", None, None, None))
    return jax.shard_map(
        per_device,
        mesh=mesh,
        in_specs=placed,
        out_specs=placed,
        check_vma=False,
    )
```

profile of v0, /device:TPU:0, one launch (start us, length us, event | category | flops | bytes accessed | tf_op | source)
XLA Modules:
  0.0 269.4 jit_solution(15582245212249587290)
XLA Ops:
  7.2 2.2 fusion.1
  9.4 1.3 collective-permute-start.4
  10.7 6.4 %collective-permute-start.5 = (f32[32,8,384]{2,1,0:T(8,128)}, f32[32,8,384]{2,1,0:T(8,128)}, u32[]{:S(2)}, u32[]{:S(2)}) collective-permute-start(f32[32,8,384]{2,1,0:T(8,128)} %get-tuple-element.13), channel_id=1, source_target_pairs={{0,2},{2,4},{4,6},{6,8},{8,10},{10,12},{12,14},{1,3},{3,5},{5,7},{... | collective-permute-start | bytes 1179656 | tf_op jit(solution)/shard_map/ppermute | solution.py:252
  17.1 2.1 fusion.3
  19.2 1.3 collective-permute-start
  20.5 5.5 %collective-permute-start.1 = (f32[32,8,384]{2,1,0:T(8,128)}, f32[32,8,384]{2,1,0:T(8,128)}, u32[]{:S(2)}, u32[]{:S(2)}) collective-permute-start(f32[32,8,384]{2,1,0:T(8,128)} %get-tuple-element.17), channel_id=1, source_target_pairs={{0,2},{2,4},{4,6},{6,8},{8,10},{10,12},{12,14},{1,3},{3,5},{5,7},{... | collective-permute-start | bytes 1179656 | tf_op jit(solution)/shard_map/ppermute | solution.py:252
  26.0 1.1 fusion
  30.1 1.6 dynamic-slice_bitcast_fusion.1.bz_ref
  31.6 1.3 dynamic-slice_bitcast_fusion.2.by_ref
  33.7 1.9 dynamic-slice_bitcast_fusion.bz_ref
  35.6 1.0 constant_dynamic-update-slice_fusion.3
  36.7 4.1 %collective-permute-done.5 = f32[32,8,384]{2,1,0:T(8,128)} collective-permute-done((f32[32,8,384]{2,1,0:T(8,128)}, f32[32,8,384]{2,1,0:T(8,128)}, u32[]{:S(2)}, u32[]{:S(2)}) %collective-permute-start.5) | collective-permute-done | bytes 393248 | tf_op jit(solution)/shard_map/ppermute | solution.py:252
  42.2 1.3 collective-permute-start.6
  43.8 3.0 %collective-permute-start.7 = (f32[32,48,8]{1,2,0:T(8,128)S(1)}, f32[32,48,8]{1,2,0:T(8,128)S(1)}, u32[]{:S(2)}, u32[]{:S(2)}) collective-permute-start(f32[32,48,8]{1,2,0:T(8,128)S(1)} %pad_maximum_fusion.5), channel_id=1, source_target_pairs={{0,1},{2,3},{4,5},{6,7},{8,9},{10,11},{12,13},{14,15},{16,17},{18,... | collective-permute-start | bytes 147464 | tf_op jit(solution)/shard_map/ppermute | solution.py:260
  46.8 1.0 constant_dynamic-update-slice_fusion.1
  47.9 1.3 collective-permute-done.1
  50.5 1.3 collective-permute-start.2
  52.1 3.0 %collective-permute-start.3 = (f32[32,48,8]{1,2,0:T(8,128)S(1)}, f32[32,48,8]{1,2,0:T(8,128)S(1)}, u32[]{:S(2)}, u32[]{:S(2)}) collective-permute-start(f32[32,48,8]{1,2,0:T(8,128)S(1)} %pad_maximum_fusion.3), channel_id=1, source_target_pairs={{0,1},{2,3},{4,5},{6,7},{8,9},{10,11},{12,13},{14,15},{16,17},{18,... | collective-permute-start | bytes 147464 | tf_op jit(solution)/shard_map/ppermute | solution.py:260
  55.1 1.3 dynamic-slice_bitcast_fusion.3.by_ref
  58.4 1.6 pad_maximum_fusion.1
  60.1 48.0 %transport.2.adj_ref = f32[32,32,384]{2,1,0:T(8,128)} custom-call(f32[16,32,128]{2,1,0:T(8,128)} %pad.7.v_ref, f32[32,16]{1,0:T(8,128)} %constant.51.clone.bx_ref, bf16[48,96]{1,0:T(8,128)(2,1)} %dynamic-slice_bitcast_fusion.2.by_ref, bf16[128,512]{1,0:T(8,128)(2,1)} %dynamic-slice_bitcast_fusion.1.bz_ref, f32[32,32,384]{2,1,0:T(8,128)} %q_ref.3, ...), custom_call_target="tpu_custom_call" | custom-call | flops 157286400 | bytes 60000000 | tf_op jit(solution)/shard_map/transport/pallas_call | solution.py:336
  108.1 11.9 %project.1 = f32[16,32,128]{2,1,0:T(8,128)} custom-call(f32[32,32,384]{2,1,0:T(8,128)} %transport.2.adj_ref, f32[32,32,384]{2,1,0:T(8,128)} %q_ref.5, f32[32,16,384]{2,1,0:T(8,128)} %copy-done.1, f32[32,48,128]{2,1,0:T(8,128)} %get-tuple-element.23.zt_ref, f32[32,16]{1,0:T(8,128)} %constant.51.clone.bx_ref, ...), custom_call_target="tpu_custom_call" | custom-call | tf_op jit(solution)/shard_map/project/pallas_call | solution.py:339
  120.0 91.4 %all-reduce.4.cloned.1.call-done = f32[16,32,96]{2,1,0:T(8,128)} async-done(((f32[16,32,96]{2,1,0:T(8,128)}), f32[16,32,96]{2,1,0:T(8,128)}) %all-reduce.4.cloned.1.call-update) | async-done | bytes 196624 | tf_op jit(solution)/shard_map/psum | solution.py:340
  213.2 48.0 %transport.3 = f32[32,32,384]{2,1,0:T(8,128)} custom-call(f32[16,32,128]{2,1,0:T(8,128)} %pad.8.v_ref, f32[32,16]{1,0:T(8,128)} %constant.51.clone.bx_ref, bf16[48,96]{1,0:T(8,128)(2,1)} %dynamic-slice_bitcast_fusion.2.by_ref, bf16[128,512]{1,0:T(8,128)(2,1)} %dynamic-slice_bitcast_fusion.1.bz_ref, f32[32,32,384]{2,1,0:T(8,128)} %q_ref.5, ...), custom_call_target="tpu_custom_call" | custom-call | flops 157286400 | bytes 60000000 | tf_op jit(solution)/shard_map/transport/pallas_call | solution.py:342
  (59 shorter events, 12.1 us)
Async XLA Ops:
  7.2 18.8 %copy-start = (f32[32,32,384]{2,1,0:T(8,128)S(1)}, f32[32,32,384]{2,1,0:T(8,128)}, u32[]{:S(2)}) copy-start(f32[32,32,384]{2,1,0:T(8,128)} %q_ref.5) | copy-start | bytes 4718596
  7.2 204.2 %all-reduce.4.cloned.1.call-start = ((), (), s32[]{:S(2)}) async-start(), calls=%async_computation | async-start | bytes 524288 | tf_op jit(solution)/shard_map/psum | solution.py:340
  9.4 26.3 %collective-permute-start.4 = (f32[32,8,384]{2,1,0:T(8,128)}, f32[32,8,384]{2,1,0:T(8,128)}, u32[]{:S(2)}, u32[]{:S(2)}) collective-permute-start(f32[32,8,384]{2,1,0:T(8,128)} %get-tuple-element.14), channel_id=1, source_target_pairs={{2,0},{4,2},{6,4},{8,6},{10,8},{12,10},{14,12},{3,1},{5,3},{7,5},{... | collective-permute-start | bytes 1179656 | tf_op jit(solution)/shard_map/ppermute | solution.py:253
  10.7 16.4 %copy-start.2 = (f32[32,32,384]{2,1,0:T(8,128)S(1)}, f32[32,32,384]{2,1,0:T(8,128)}, u32[]{:S(2)}) copy-start(f32[32,32,384]{2,1,0:T(8,128)} %q_ref.3) | copy-start | bytes 4718596
  10.7 30.1 %collective-permute-start.5 = (f32[32,8,384]{2,1,0:T(8,128)}, f32[32,8,384]{2,1,0:T(8,128)}, u32[]{:S(2)}, u32[]{:S(2)}) collective-permute-start(f32[32,8,384]{2,1,0:T(8,128)} %get-tuple-element.13), channel_id=1, source_target_pairs={{0,2},{2,4},{4,6},{6,8},{8,10},{10,12},{12,14},{1,3},{3,5},{5,7},{... | collective-permute-start | bytes 1179656 | tf_op jit(solution)/shard_map/ppermute | solution.py:252
  19.2 27.6 %collective-permute-start = (f32[32,8,384]{2,1,0:T(8,128)}, f32[32,8,384]{2,1,0:T(8,128)}, u32[]{:S(2)}, u32[]{:S(2)}) collective-permute-start(f32[32,8,384]{2,1,0:T(8,128)} %get-tuple-element.18), channel_id=1, source_target_pairs={{2,0},{4,2},{6,4},{8,6},{10,8},{12,10},{14,12},{3,1},{5,3},{7,5},{... | collective-permute-start | bytes 1179656 | tf_op jit(solution)/shard_map/ppermute | solution.py:253
  20.5 28.6 %collective-permute-start.1 = (f32[32,8,384]{2,1,0:T(8,128)}, f32[32,8,384]{2,1,0:T(8,128)}, u32[]{:S(2)}, u32[]{:S(2)}) collective-permute-start(f32[32,8,384]{2,1,0:T(8,128)} %get-tuple-element.17), channel_id=1, source_target_pairs={{0,2},{2,4},{4,6},{6,8},{8,10},{10,12},{12,14},{1,3},{3,5},{5,7},{... | collective-permute-start | bytes 1179656 | tf_op jit(solution)/shard_map/ppermute | solution.py:252
  27.1 1.3 copy-start.8
  28.4 4.6 %copy-start.6 = (f32[32,32,8]{2,1,0:T(8,128)S(1)}, f32[32,32,8]{2,1,0:T(8,128)}, u32[]{:S(2)}) copy-start(f32[32,32,8]{2,1,0:T(8,128)} %get-tuple-element.11) | copy-start | bytes 98308
  28.9 4.2 %copy-start.5 = (f32[32,32,8]{2,1,0:T(8,128)S(1)}, f32[32,32,8]{2,1,0:T(8,128)}, u32[]{:S(2)}) copy-start(f32[32,32,8]{2,1,0:T(8,128)} %get-tuple-element.12) | copy-start | bytes 98308
  28.9 4.4 %copy-start.4 = (f32[32,32,8]{2,1,0:T(8,128)S(1)}, f32[32,32,8]{2,1,0:T(8,128)}, u32[]{:S(2)}) copy-start(f32[32,32,8]{2,1,0:T(8,128)} %get-tuple-element.15) | copy-start | bytes 98308
  41.8 6.0 %copy-start.1 = (f32[32,16,384]{2,1,0:T(8,128)}, f32[32,16,384]{2,1,0:T(8,128)S(1)}, u32[]{:S(2)}) copy-start(f32[32,16,384]{2,1,0:T(8,128)S(1)} %constant_dynamic-update-slice_fusion.2.yh_ref) | copy-start | bytes 2359300
  42.2 15.0 %collective-permute-start.6 = (f32[32,48,8]{1,2,0:T(8,128)S(1)}, f32[32,48,8]{1,2,0:T(8,128)S(1)}, u32[]{:S(2)}, u32[]{:S(2)}) collective-permute-start(f32[32,48,8]{1,2,0:T(8,128)S(1)} %pad_maximum_fusion.4), channel_id=1, source_target_pairs={{1,0},{3,2},{5,4},{7,6},{9,8},{11,10},{13,12},{15,14},{17,16},{19,... | collective-permute-start | bytes 147464 | tf_op jit(solution)/shard_map/ppermute | solution.py:261
  43.8 13.8 %collective-permute-start.7 = (f32[32,48,8]{1,2,0:T(8,128)S(1)}, f32[32,48,8]{1,2,0:T(8,128)S(1)}, u32[]{:S(2)}, u32[]{:S(2)}) collective-permute-start(f32[32,48,8]{1,2,0:T(8,128)S(1)} %pad_maximum_fusion.5), channel_id=1, source_target_pairs={{0,1},{2,3},{4,5},{6,7},{8,9},{10,11},{12,13},{14,15},{16,17},{18,... | collective-permute-start | bytes 147464 | tf_op jit(solution)/shard_map/ppermute | solution.py:260
  47.9 8.6 %copy-start.7 = (f32[16,32,96]{2,1,0:T(8,128)S(1)}, f32[16,32,96]{2,1,0:T(8,128)}, u32[]{:S(2)}) copy-start(f32[16,32,96]{2,1,0:T(8,128)} %broadcast_multiply_fusion.1) | copy-start | bytes 589828
  50.2 7.0 %copy-start.3 = (f32[32,16,384]{2,1,0:T(8,128)}, f32[32,16,384]{2,1,0:T(8,128)S(1)}, u32[]{:S(2)}) copy-start(f32[32,16,384]{2,1,0:T(8,128)S(1)} %constant_dynamic-update-slice_fusion.yh_ref) | copy-start | bytes 2359300
  50.5 7.3 %collective-permute-start.2 = (f32[32,48,8]{1,2,0:T(8,128)S(1)}, f32[32,48,8]{1,2,0:T(8,128)S(1)}, u32[]{:S(2)}, u32[]{:S(2)}) collective-permute-start(f32[32,48,8]{1,2,0:T(8,128)S(1)} %pad_maximum_fusion.2), channel_id=1, source_target_pairs={{1,0},{3,2},{5,4},{7,6},{9,8},{11,10},{13,12},{15,14},{17,16},{19,... | collective-permute-start | bytes 147464 | tf_op jit(solution)/shard_map/ppermute | solution.py:261
  52.1 6.1 %collective-permute-start.3 = (f32[32,48,8]{1,2,0:T(8,128)S(1)}, f32[32,48,8]{1,2,0:T(8,128)S(1)}, u32[]{:S(2)}, u32[]{:S(2)}) collective-permute-start(f32[32,48,8]{1,2,0:T(8,128)S(1)} %pad_maximum_fusion.3), channel_id=1, source_target_pairs={{0,1},{2,3},{4,5},{6,7},{8,9},{10,11},{12,13},{14,15},{16,17},{18,... | collective-permute-start | bytes 147464 | tf_op jit(solution)/shard_map/ppermute | solution.py:260
  108.1 103.3 %copy-start.9 = (f32[16,32,96]{2,1,0:T(8,128)S(1)}, f32[16,32,96]{2,1,0:T(8,128)}, u32[]{:S(2)}) copy-start(f32[16,32,96]{2,1,0:T(8,128)} %constant.52.clone) | copy-start | bytes 589828
Sparse Core Ops, SparseCore 0:
  120.1 91.2 all-reduce.3
where the time goes:
time: 270 us; the launch traced here: 269 us
  Pallas kernels  108 us (40%)
  waiting for transfers between devices  96.8 us (36%)
  local copies, waits for them, and re-layouts  23.3 us (9%)
  starting transfers between devices  23.1 us (9%)
  between operations  14.3 us (5%)
  other arithmetic  3.84 us (1%)
    psum x1, waiting for transfers between devices, per_device(): summed = lax.psum(partial[:, :, :3 * modes], ('ha', 'dev'))  91.4 us
    pallas_call x1, Pallas kernels, per_device(): transport(widen(updated * scale), bx, by_wide, bz_wide, brain_image, *ima...  48 us
    pallas_call x1, Pallas kernels, per_device(): transport(widen(old * -scale), bx, by_wide, bz_wide, adjoint_field, *adjo...  48 us
    pallas_call x1, Pallas kernels, per_device(): project(adjoint_end, brain_image, *image_halo, bx, by_back, bz_back)  11.9 us
    ppermute x2, starting transfers between devices, halo_of(): before = lax.ppermute(field[:, -HALO:, :], 'ha', forward)  11.9 us
    squeeze x4, local copies, waits for them, and re-layouts, pick(): lax.dynamic_index_in_dim(jnp.asarray(np.stack(tables)), index, 0, keepdim...  6.09 us
    ppermute x2, starting transfers between devices, halo_of(): left = lax.ppermute(tail, 'dev', forward)  6.08 us
    ppermute x2, waiting for transfers between devices, halo_of(): before = lax.ppermute(field[:, -HALO:, :], 'ha', forward)  5.4 us
  transfers between devices with their start and end apart: 9, of which 3 were waited for; matrix products, arithmetic and copies ran while one was open for 7% of the time, Pallas kernels for 0%

commit v1 on v0

--- a/solution.py
+++ b/solution.py
@@ -240,6 +240,58 @@
     lax.fori_loop(0, modes_x, finish, 0)
 
 
+def peer_of(index, sides):
+    return {"ha": index // sides, "dev": lax.rem(index, sides)}
+
+
+def update_kernel(count, sides, part_ref, old_ref, factor_ref, out_ref, held, send, recv, send2, recv2):
+    me = lax.axis_index("ha") * sides + lax.axis_index("dev")
+    rows = held.shape[1]
+    barrier = pltpu.get_barrier_semaphore()
+    for d in range(1, count):
+        peer = lax.rem(me + d, count)
+        pl.semaphore_signal(
+            barrier, inc=1, device_id=peer_of(peer, sides), device_id_type=pl.DeviceIdType.MESH
+        )
+    pl.semaphore_wait(barrier, count - 1)
+    mine = pl.ds(pl.multiple_of(me * rows, rows), rows)
+    copies = []
+    for d in range(1, count):
+        peer = lax.rem(me + d, count)
+        copy = pltpu.make_async_remote_copy(
+            src_ref=part_ref.at[pl.ds(pl.multiple_of(peer * rows, rows), rows)],
+            dst_ref=held.at[d],
+            send_sem=send.at[d],
+            recv_sem=recv.at[d],
+            device_id=peer_of(peer, sides),
+            device_id_type=pl.DeviceIdType.MESH,
+        )
+        copy.start()
+        copies.append(copy)
+    total = part_ref[mine]
+    for d in range(1, count):
+        copies[d - 1].wait_recv()
+        total = total + held[d]
+    out_ref[mine] = old_ref[mine] + factor_ref[mine] * total
+    for copy in copies:
+        copy.wait_send()
+    copies = []
+    for d in range(1, count):
+        peer = lax.rem(me + d, count)
+        copy = pltpu.make_async_remote_copy(
+            src_ref=out_ref.at[mine],
+            dst_ref=out_ref.at[mine],
+            send_sem=send2.at[d],
+            recv_sem=recv2.at[d],
+            device_id=peer_of(peer, sides),
+            device_id_type=pl.DeviceIdType.MESH,
+        )
+        copy.start()
+        copies.append(copy)
+    for copy in copies:
+        copy.wait()
+
+
 VMEM = pl.BlockSpec(memory_space=pltpu.VMEM)
 SMEM = pl.BlockSpec(memory_space=pltpu.SMEM)
 PARAMS = pltpu.CompilerParams(vmem_limit_bytes=60 * 1024 * 1024)
@@ -297,7 +349,7 @@
     bz_wide, bz_back = pick(expand_z, index_z), pick(project_z, index_z)
     bx = jnp.asarray(basis(np.arange(planes), planes, modes_x))
     factor = mode_factor((planes, height, depth), (modes_x, modes, modes))
-    factor = np.tile(factor, (1, 1, 3)).astype(np.float32)
+    factor = np.tile(factor, (1, 1, LANES // modes)).astype(np.float32).reshape(-1, LANES)
     scale = 1.0 / math.sqrt(modes_x * modes * modes)
 
     def widen(value):
@@ -330,17 +382,29 @@
         name="project",
     )
 
-    old = velocity_modes.transpose(1, 2, 0, 3).reshape(modes_x, modes, 3 * modes)
+    devices = count_y * count_z
+    entries = modes_x * modes
+    update = pl.pallas_call(
+        functools.partial(update_kernel, devices, count_z),
+        out_shape=jax.ShapeDtypeStruct((entries, LANES), F32),
+        in_specs=[VMEM, VMEM, VMEM],
+        out_specs=VMEM,
+        scratch_shapes=[pltpu.VMEM((devices, entries // devices, LANES), F32)]
+        + [pltpu.SemaphoreType.DMA((devices,))] * 4,
+        compiler_params=pltpu.CompilerParams(collective_id=0, has_side_effects=True),
+        name="update",
+    )
+
+    old = widen(velocity_modes.transpose(1, 2, 0, 3).reshape(modes_x, modes, 3 * modes))
     adjoint_halo = halo_of(adjoint_field)
     image_halo = halo_of(brain_image)
-    adjoint_end = transport(
-        widen(old * -scale), bx, by_wide, bz_wide, adjoint_field, *adjoint_halo
-    )
+    adjoint_end = transport(old, bx * -scale, by_wide, bz_wide, adjoint_field, *adjoint_halo)
     partial = project(adjoint_end, brain_image, *image_halo, bx, by_back, bz_back)
-    summed = lax.psum(partial[:, :, : 3 * modes], ("ha", "dev"))
-    updated = old + factor * summed
-    image_end = transport(widen(updated * scale), bx, by_wide, bz_wide, brain_image, *image_halo)
-    velocity_next = updated.reshape(modes_x, modes, 3, modes).transpose(2, 0, 1, 3)
+    updated = update(partial.reshape(entries, LANES), old.reshape(entries, LANES), factor)
+    updated = updated.reshape(modes_x, modes, LANES)
+    image_end = transport(updated, bx * scale, by_wide, bz_wide, brain_image, *image_halo)
+    velocity_next = updated[:, :, : 3 * modes].reshape(modes_x, modes, 3, modes)
+    velocity_next = velocity_next.transpose(2, 0, 1, 3)
     return (adjoint_end, image_end, velocity_next)
 
 

time: 270 us -> 184 us (0.68)
  waiting for transfers between devices: 96.8 us -> 11 us
  Pallas kernels: 108 us -> 127 us
  between operations: 14.3 us -> 0.94 us
  local copies, waits for them, and re-layouts: 23.3 us -> 19.3 us
    psum x1 -> x0, waiting for transfers between devices: 91.4 us -> none  [per_device(): summed = lax.psum(partial[:, :, :3 * modes], ('ha', 'dev'))]
    pallas_call x2 -> x3, Pallas kernels: 96.1 us -> 115 us  [the longest x1 48.1 us: per_device(): transport(updated, bx * scale, by_wide, bz_wide, brain_image, *image_halo)]
    ppermute x2, waiting for transfers between devices: 5.4 us -> 11 us  [halo_of(): before = lax.ppermute(field[:, -HALO:, :], 'ha', forward)]
  transfers between devices with their start and end apart: 9 -> 8, of which waited for: 3 -> 2; matrix products, arithmetic and copies ran while one was open for 7% -> 8% of each run, Pallas kernels for 0% -> 0%
where the time goes in v1:
time: 184 us; the launch traced here: 183 us
  Pallas kernels  127 us (69%)
  starting transfers between devices  23 us (12%)
  local copies, waits for them, and re-layouts  19.3 us (10%)
  waiting for transfers between devices  11 us (6%)
  other arithmetic  2.11 us (1%)
    pallas_call x1, Pallas kernels, per_device(): transport(updated, bx * scale, by_wide, bz_wide, brain_image, *image_halo)  48.1 us
    pallas_call x1, Pallas kernels, per_device(): transport(old, bx * -scale, by_wide, bz_wide, adjoint_field, *adjoint_halo)  48 us
    pallas_call x1, Pallas kernels, per_device(): update(partial.reshape(entries, LANES), old.reshape(entries, LANES), factor)  19.1 us
    pallas_call x1, Pallas kernels, per_device(): project(adjoint_end, brain_image, *image_halo, bx, by_back, bz_back)  11.8 us
    ppermute x2, starting transfers between devices, halo_of(): before = lax.ppermute(field[:, -HALO:, :], 'ha', forward)  11.1 us
    ppermute x2, waiting for transfers between devices, halo_of(): before = lax.ppermute(field[:, -HALO:, :], 'ha', forward)  11 us
    ppermute x2, starting transfers between devices, halo_of(): left = lax.ppermute(tail, 'dev', forward)  6.73 us
    squeeze x4, local copies, waits for them, and re-layouts, pick(): lax.dynamic_index_in_dim(jnp.asarray(np.stack(tables)), index, 0, keepdim...  6.11 us
  transfers between devices with their start and end apart: 8, of which 2 were waited for; matrix products, arithmetic and copies ran while one was open for 8% of the time, Pallas kernels for 0%

profile of v1, /device:TPU:0, one launch (start us, length us, event | category | flops | bytes accessed | tf_op | source)
XLA Modules:
  0.0 183.4 jit_solution(16727200140405842992)
XLA Ops:
  0.6 2.2 %fusion.1 = (f32[32,8,384]{2,1,0:T(8,128)}, f32[32,8,384]{2,1,0:T(8,128)}) fusion(f32[32,32,384]{2,1,0:T(8,128)} %q_ref.5), kind=kLoop, calls=%fused_computation.15 | loop fusion | bytes 1572864 | tf_op jit(solution)/shard_map/slice | solution.py:304
  2.8 1.3 collective-permute-start.4
  4.1 5.7 %collective-permute-start.5 = (f32[32,8,384]{2,1,0:T(8,128)}, f32[32,8,384]{2,1,0:T(8,128)S(1)}, u32[]{:S(2)}, u32[]{:S(2)}) collective-permute-start(f32[32,8,384]{2,1,0:T(8,128)} %get-tuple-element.11), channel_id=1, source_target_pairs={{0,2},{2,4},{4,6},{6,8},{8,10},{10,12},{12,14},{1,3},{3,5},{5,7},{... | collective-permute-start | bytes 1179656 | tf_op jit(solution)/shard_map/ppermute | solution.py:304
  9.8 2.0 %fusion.3 = (f32[32,8,384]{2,1,0:T(8,128)}, f32[32,8,384]{2,1,0:T(8,128)}) fusion(f32[32,32,384]{2,1,0:T(8,128)} %q_ref.3), kind=kLoop, calls=%fused_computation.17 | loop fusion | bytes 1572864 | tf_op jit(solution)/shard_map/slice | solution.py:304
  11.8 1.3 collective-permute-start
  13.1 5.4 %collective-permute-start.1 = (f32[32,8,384]{2,1,0:T(8,128)}, f32[32,8,384]{2,1,0:T(8,128)S(1)}, u32[]{:S(2)}, u32[]{:S(2)}) collective-permute-start(f32[32,8,384]{2,1,0:T(8,128)} %get-tuple-element.15), channel_id=1, source_target_pairs={{0,2},{2,4},{4,6},{6,8},{8,10},{10,12},{12,14},{1,3},{3,5},{5,7},{... | collective-permute-start | bytes 1179656 | tf_op jit(solution)/shard_map/ppermute | solution.py:304
  18.6 1.0 fusion
  19.8 1.6 dynamic-slice_bitcast_fusion.1.bz_ref
  21.4 1.3 dynamic-slice_bitcast_fusion.2.by_ref
  23.5 1.9 %dynamic-slice_bitcast_fusion.bz_ref = bf16[1152,256]{1,0:T(8,128)(2,1)} fusion(bf16[2,1152,256]{2,1,0:T(8,128)(2,1)} %constant.50.clone, s32[]{:T(128)S(6)} %select_n.13), kind=kLoop, calls=%fused_computation.2 | loop fusion | bytes 1179652 | tf_op jit(solution)/shard_map/jit(dynamic_index_in_dim)/squeeze | solution.py:346
  25.4 1.0 constant_dynamic-update-slice_fusion.3
  26.4 7.8 %collective-permute-done.5 = f32[32,8,384]{2,1,0:T(8,128)S(1)} collective-permute-done((f32[32,8,384]{2,1,0:T(8,128)}, f32[32,8,384]{2,1,0:T(8,128)S(1)}, u32[]{:S(2)}, u32[]{:S(2)}) %collective-permute-start.5) | collective-permute-done | bytes 393248 | tf_op jit(solution)/shard_map/ppermute | solution.py:304
  34.6 1.3 collective-permute-start.6
  36.2 3.0 %collective-permute-start.7 = (f32[32,48,8]{1,2,0:T(8,128)S(1)}, f32[32,48,8]{1,2,0:T(8,128)S(1)}, u32[]{:S(2)}, u32[]{:S(2)}) collective-permute-start(f32[32,48,8]{1,2,0:T(8,128)S(1)} %pad_maximum_fusion.5), channel_id=1, source_target_pairs={{0,1},{2,3},{4,5},{6,7},{8,9},{10,11},{12,13},{14,15},{16,17},{18,... | collective-permute-start | bytes 147464 | tf_op jit(solution)/shard_map/ppermute | solution.py:312
  39.3 3.3 %collective-permute-done.1 = f32[32,8,384]{2,1,0:T(8,128)S(1)} collective-permute-done((f32[32,8,384]{2,1,0:T(8,128)}, f32[32,8,384]{2,1,0:T(8,128)S(1)}, u32[]{:S(2)}, u32[]{:S(2)}) %collective-permute-start.1) | collective-permute-done | bytes 393248 | tf_op jit(solution)/shard_map/ppermute | solution.py:304
  43.0 1.3 collective-permute-start.2
  44.5 3.7 %collective-permute-start.3 = (f32[32,48,8]{1,2,0:T(8,128)S(1)}, f32[32,48,8]{1,2,0:T(8,128)}, u32[]{:S(2)}, u32[]{:S(2)}) collective-permute-start(f32[32,48,8]{1,2,0:T(8,128)S(1)} %pad_maximum_fusion.3), channel_id=1, source_target_pairs={{0,1},{2,3},{4,5},{6,7},{8,9},{10,11},{12,13},{14,15},{16,17},{18,... | collective-permute-start | bytes 147464 | tf_op jit(solution)/shard_map/ppermute | solution.py:312
  48.2 1.3 dynamic-slice_bitcast_fusion.3.by_ref
  52.2 1.2 copy.22
  53.3 1.6 pad_maximum_fusion.1
  55.0 48.0 %transport.2.adj_ref = f32[32,32,384]{2,1,0:T(8,128)} custom-call(f32[16,32,128]{2,1,0:T(8,128)} %pad.4.v_ref, f32[32,16]{1,0:T(8,128)} %constant.56.bx_ref, bf16[48,96]{1,0:T(8,128)(2,1)} %dynamic-slice_bitcast_fusion.2.by_ref, bf16[128,512]{1,0:T(8,128)(2,1)} %dynamic-slice_bitcast_fusion.1.bz_ref, f32[32,32,384]{2,1,0:T(8,128)} %q_ref.3, ...), custom_call_target="tpu_custom_call" | custom-call | flops 157286400 | bytes 60000000 | tf_op jit(solution)/shard_map/transport/pallas_call | solution.py:401
  103.0 11.8 %project.1 = f32[16,32,128]{2,1,0:T(8,128)} custom-call(f32[32,32,384]{2,1,0:T(8,128)} %transport.2.adj_ref, f32[32,32,384]{2,1,0:T(8,128)} %q_ref.5, f32[32,16,384]{2,1,0:T(8,128)} %copy-done.1, f32[32,48,128]{2,1,0:T(8,128)} %get-tuple-element.21.zt_ref, f32[32,16]{1,0:T(8,128)} %constant.51.clone.bx_ref, ...), custom_call_target="tpu_custom_call" | custom-call | tf_op jit(solution)/shard_map/project/pallas_call | solution.py:402
  114.9 19.1 %update.1 = f32[512,128]{1,0:T(8,128)} custom-call(f32[512,128]{1,0:T(8,128)} %bitcast.18, f32[512,128]{1,0:T(8,128)} %bitcast.15, f32[512,128]{1,0:T(8,128)} %constant.52.clone.factor_ref), custom_call_target="tpu_custom_call" | custom-call | tf_op jit(solution)/shard_map/update/pallas_call | solution.py:403
  134.0 48.1 %transport.3 = f32[32,32,384]{2,1,0:T(8,128)} custom-call(f32[16,32,128]{2,1,0:T(8,128)} %bitcast.16, f32[32,16]{1,0:T(8,128)} %constant.57.bx_ref, bf16[48,96]{1,0:T(8,128)(2,1)} %dynamic-slice_bitcast_fusion.2.by_ref, bf16[128,512]{1,0:T(8,128)(2,1)} %dynamic-slice_bitcast_fusion.1.bz_ref, f32[32,32,384]{2,1,0:T(8,128)} %q_ref.5, ...), custom_call_target="tpu_custom_call" | custom-call | flops 157286400 | bytes 60000000 | tf_op jit(solution)/shard_map/transport/pallas_call | solution.py:405
  (48 shorter events, 6.2 us)
Async XLA Ops:
  0.6 18.0 %copy-start = (f32[32,32,384]{2,1,0:T(8,128)S(1)}, f32[32,32,384]{2,1,0:T(8,128)}, u32[]{:S(2)}) copy-start(f32[32,32,384]{2,1,0:T(8,128)} %q_ref.5) | copy-start | bytes 4718596
  2.8 22.6 %collective-permute-start.4 = (f32[32,8,384]{2,1,0:T(8,128)}, f32[32,8,384]{2,1,0:T(8,128)}, u32[]{:S(2)}, u32[]{:S(2)}) collective-permute-start(f32[32,8,384]{2,1,0:T(8,128)} %get-tuple-element.12), channel_id=1, source_target_pairs={{2,0},{4,2},{6,4},{8,6},{10,8},{12,10},{14,12},{3,1},{5,3},{7,5},{... | collective-permute-start | bytes 1179656 | tf_op jit(solution)/shard_map/ppermute | solution.py:305
  4.1 15.5 %copy-start.2 = (f32[32,32,384]{2,1,0:T(8,128)S(1)}, f32[32,32,384]{2,1,0:T(8,128)}, u32[]{:S(2)}) copy-start(f32[32,32,384]{2,1,0:T(8,128)} %q_ref.3) | copy-start | bytes 4718596
  4.1 30.1 %collective-permute-start.5 = (f32[32,8,384]{2,1,0:T(8,128)}, f32[32,8,384]{2,1,0:T(8,128)S(1)}, u32[]{:S(2)}, u32[]{:S(2)}) collective-permute-start(f32[32,8,384]{2,1,0:T(8,128)} %get-tuple-element.11), channel_id=1, source_target_pairs={{0,2},{2,4},{4,6},{6,8},{8,10},{10,12},{12,14},{1,3},{3,5},{5,7},{... | collective-permute-start | bytes 1179656 | tf_op jit(solution)/shard_map/ppermute | solution.py:304
  11.8 27.4 %collective-permute-start = (f32[32,8,384]{2,1,0:T(8,128)}, f32[32,8,384]{2,1,0:T(8,128)S(1)}, u32[]{:S(2)}, u32[]{:S(2)}) collective-permute-start(f32[32,8,384]{2,1,0:T(8,128)} %get-tuple-element.16), channel_id=1, source_target_pairs={{2,0},{4,2},{6,4},{8,6},{10,8},{12,10},{14,12},{3,1},{5,3},{7,5},{... | collective-permute-start | bytes 1179656 | tf_op jit(solution)/shard_map/ppermute | solution.py:305
  13.1 29.4 %collective-permute-start.1 = (f32[32,8,384]{2,1,0:T(8,128)}, f32[32,8,384]{2,1,0:T(8,128)S(1)}, u32[]{:S(2)}, u32[]{:S(2)}) collective-permute-start(f32[32,8,384]{2,1,0:T(8,128)} %get-tuple-element.15), channel_id=1, source_target_pairs={{0,2},{2,4},{4,6},{6,8},{8,10},{10,12},{12,14},{1,3},{3,5},{5,7},{... | collective-permute-start | bytes 1179656 | tf_op jit(solution)/shard_map/ppermute | solution.py:304
  19.6 3.3 %copy-start.5 = (f32[32,32,8]{2,1,0:T(8,128)S(1)}, f32[32,32,8]{2,1,0:T(8,128)}, u32[]{:S(2)}) copy-start(f32[32,32,8]{2,1,0:T(8,128)} %get-tuple-element.10) | copy-start | bytes 98308
  34.2 5.0 %copy-start.1 = (f32[32,16,384]{2,1,0:T(8,128)}, f32[32,16,384]{2,1,0:T(8,128)S(1)}, u32[]{:S(2)}) copy-start(f32[32,16,384]{2,1,0:T(8,128)S(1)} %constant_dynamic-update-slice_fusion.2.yh_ref) | copy-start | bytes 2359300
  34.6 16.6 %collective-permute-start.6 = (f32[32,48,8]{1,2,0:T(8,128)S(1)}, f32[32,48,8]{1,2,0:T(8,128)S(1)}, u32[]{:S(2)}, u32[]{:S(2)}) collective-permute-start(f32[32,48,8]{1,2,0:T(8,128)S(1)} %pad_maximum_fusion.4), channel_id=1, source_target_pairs={{1,0},{3,2},{5,4},{7,6},{9,8},{11,10},{13,12},{15,14},{17,16},{19,... | collective-permute-start | bytes 147464 | tf_op jit(solution)/shard_map/ppermute | solution.py:313
  36.2 15.4 %collective-permute-start.7 = (f32[32,48,8]{1,2,0:T(8,128)S(1)}, f32[32,48,8]{1,2,0:T(8,128)S(1)}, u32[]{:S(2)}, u32[]{:S(2)}) collective-permute-start(f32[32,48,8]{1,2,0:T(8,128)S(1)} %pad_maximum_fusion.5), channel_id=1, source_target_pairs={{0,1},{2,3},{4,5},{6,7},{8,9},{10,11},{12,13},{14,15},{16,17},{18,... | collective-permute-start | bytes 147464 | tf_op jit(solution)/shard_map/ppermute | solution.py:312
  39.3 10.2 %copy-start.6 = (f32[3,16,32,32]{3,2,1,0:T(8,128)S(1)}, f32[3,16,32,32]{3,2,1,0:T(8,128)}, u32[]{:S(2)}) copy-start(f32[3,16,32,32]{3,2,1,0:T(8,128)} %param.11) | copy-start | bytes 589828
  42.6 7.5 %copy-start.3 = (f32[32,16,384]{2,1,0:T(8,128)}, f32[32,16,384]{2,1,0:T(8,128)S(1)}, u32[]{:S(2)}) copy-start(f32[32,16,384]{2,1,0:T(8,128)S(1)} %constant_dynamic-update-slice_fusion.yh_ref) | copy-start | bytes 2359300
  43.0 8.9 %collective-permute-start.2 = (f32[32,48,8]{1,2,0:T(8,128)S(1)}, f32[32,48,8]{1,2,0:T(8,128)S(1)}, u32[]{:S(2)}, u32[]{:S(2)}) collective-permute-start(f32[32,48,8]{1,2,0:T(8,128)S(1)} %pad_maximum_fusion.2), channel_id=1, source_target_pairs={{1,0},{3,2},{5,4},{7,6},{9,8},{11,10},{13,12},{15,14},{17,16},{19,... | collective-permute-start | bytes 147464 | tf_op jit(solution)/shard_map/ppermute | solution.py:313
  44.5 7.6 %collective-permute-start.3 = (f32[32,48,8]{1,2,0:T(8,128)S(1)}, f32[32,48,8]{1,2,0:T(8,128)}, u32[]{:S(2)}, u32[]{:S(2)}) collective-permute-start(f32[32,48,8]{1,2,0:T(8,128)S(1)} %pad_maximum_fusion.3), channel_id=1, source_target_pairs={{0,1},{2,3},{4,5},{6,7},{8,9},{10,11},{12,13},{14,15},{16,17},{18,... | collective-permute-start | bytes 147464 | tf_op jit(solution)/shard_map/ppermute | solution.py:312
  134.0 48.1 %copy-start.4 = (f32[512,128]{1,0:T(8,128)S(1)}, f32[512,128]{1,0:T(8,128)}, u32[]{:S(2)}) copy-start(f32[512,128]{1,0:T(8,128)} %update.1) | copy-start | bytes 786436

commit v2 on v1

--- a/solution.py
+++ b/solution.py
@@ -63,6 +63,7 @@
 
 def expand_kernel(planes, modes_x, modes, v_ref, bx_ref, by_ref, bz_ref, coefs):
     height, depth = coefs[0].shape[1:]
+    by, bz = by_ref[lax.axis_index("ha")], bz_ref.at[lax.axis_index("dev")]
     group = lax.broadcasted_iota(jnp.int32, (height, LANES), 1) // modes
 
     def body(x, carry):
@@ -71,7 +72,7 @@
             weighted = weighted + bx_ref[x, a] * v_ref[a]
         high, low = split(weighted)
         rows = jnp.concatenate([high, low, high], axis=0)
-        mixed = jnp.dot(by_ref[...], rows, preferred_element_type=F32)
+        mixed = jnp.dot(by, rows, preferred_element_type=F32)
         top = mixed.astype(BF16).astype(F32)
         rest = mixed - top
         total = jnp.ones((height, depth), F32)
@@ -80,7 +81,7 @@
             second = pltpu.roll(top, ((1 - c) * modes) % LANES, 1) if c != 1 else top
             third = pltpu.roll(rest, ((2 - c) * modes) % LANES, 1) if c != 2 else rest
             left = jnp.where(group == 0, first, jnp.where(group == 1, second, third))
-            speed = jnp.dot(left.astype(BF16), bz_ref[...], preferred_element_type=F32)
+            speed = jnp.dot(left.astype(BF16), bz[...], preferred_element_type=F32)
             plus = jnp.maximum(speed, 0.0)
             minus = jnp.maximum(-speed, 0.0)
             coefs[1 + 2 * c][x] = plus
@@ -89,7 +90,7 @@
         coefs[0][x] = total
         return carry
 
-    lax.fori_loop(0, planes, body, 0)
+    lax.fori_loop(0, planes, body, 0, unroll=2)
 
 
 def gather_field(q_ref, yh_ref, zt_ref, field):
@@ -182,13 +183,13 @@
         return carry
 
     def step(i, carry):
-        lax.fori_loop(0, planes, first, 0)
-        lax.fori_loop(0, planes, second, 0)
+        lax.fori_loop(0, planes, first, 0, unroll=4)
+        lax.fori_loop(0, planes, second, 0, unroll=4)
         return carry
 
     lax.fori_loop(0, STEPS - 1, step, 0)
-    lax.fori_loop(0, planes, first, 0)
-    lax.fori_loop(0, planes, last, 0)
+    lax.fori_loop(0, planes, first, 0, unroll=4)
+    lax.fori_loop(0, planes, last, 0, unroll=4)
 
 
 def project_kernel(
@@ -197,6 +198,7 @@
     height, width = field.shape[1:]
     rows, depth = q_ref.shape[1:]
     gather_field(q_ref, yh_ref, zt_ref, field)
+    by, bz = by_ref[lax.axis_index("ha")], bz_ref.at[lax.axis_index("dev")]
 
     def body(x, carry):
         plane = field[x + 1]
@@ -219,7 +221,7 @@
     def multiply(i, carry):
         start = i * (chunk * 2 * rows)
         wide = jnp.dot(
-            forcing[pl.ds(start, chunk * 2 * rows), :], bz_ref[...], preferred_element_type=F32
+            forcing[pl.ds(start, chunk * 2 * rows), :], bz[...], preferred_element_type=F32
         )
         wide = wide[:, 0:LANES] + wide[:, LANES : 2 * LANES]
         wide = wide.reshape(chunk, 2 * rows, LANES)
@@ -234,7 +236,7 @@
             total = total + bx_ref[x, a] * inner[x]
         high, low = split(total)
         stacked = jnp.concatenate([high, low, high], axis=0)
-        out_ref[a] = jnp.dot(by_ref[...], stacked, preferred_element_type=F32)
+        out_ref[a] = jnp.dot(by, stacked, preferred_element_type=F32)
         return carry
 
     lax.fori_loop(0, modes_x, finish, 0)
@@ -242,6 +244,79 @@
 
 def peer_of(index, sides):
     return {"ha": index // sides, "dev": lax.rem(index, sides)}
+
+
+MESH = pl.DeviceIdType.MESH
+
+
+def halo_kernel(count_y, count_z, q_ref, yh_ref, zt_ref, left_ref, right_ref, send, recv):
+    me_y, me_z = lax.axis_index("ha"), lax.axis_index("dev")
+    rows, cols = q_ref.shape[1:]
+    has = (me_y < count_y - 1, me_y > 0, me_z < count_z - 1, me_z > 0)
+    peers = ({"ha": me_y + 1}, {"ha": me_y - 1}, {"dev": me_z + 1}, {"dev": me_z - 1})
+    last = slice(cols - LANES, cols)
+    first = slice(0, LANES)
+    before, after = slice(HALO, 2 * HALO), slice(0, HALO)
+    block, rim = slice(0, rows), slice(rows, rows + 2 * HALO)
+    barrier = pltpu.get_barrier_semaphore()
+    for there, peer in zip(has, peers):
+
+        @pl.when(there)
+        def _():
+            pl.semaphore_signal(barrier, inc=1, device_id=peer, device_id_type=MESH)
+
+    def copy(source, target, slot, peer):
+        return pltpu.make_async_remote_copy(
+            src_ref=source,
+            dst_ref=target,
+            send_sem=send.at[slot],
+            recv_sem=recv.at[slot],
+            device_id=peer,
+            device_id_type=MESH,
+        )
+
+    for there, target in (
+        (has[0], yh_ref.at[:, after]),
+        (has[1], yh_ref.at[:, before]),
+        (has[2], right_ref),
+        (has[3], left_ref),
+    ):
+
+        @pl.when(jnp.logical_not(there))
+        def _():
+            target[...] = jnp.zeros(target.shape, F32)
+
+    known = sum(jnp.where(there, 1, 0) for there in has)
+    pl.semaphore_wait(barrier, known)
+
+    rows_next = copy(q_ref.at[:, rows - HALO : rows], yh_ref.at[:, before], 0, peers[0])
+    rows_prev = copy(q_ref.at[:, 0:HALO], yh_ref.at[:, after], 1, peers[1])
+    tile_next = copy(q_ref.at[:, :, last], left_ref.at[:, block], 2, peers[2])
+    tile_prev = copy(q_ref.at[:, :, first], right_ref.at[:, block], 3, peers[3])
+    rim_next = copy(yh_ref.at[:, :, last], left_ref.at[:, rim], 4, peers[2])
+    rim_prev = copy(yh_ref.at[:, :, first], right_ref.at[:, rim], 5, peers[3])
+
+    def each(pairs):
+        for there, action in pairs:
+
+            @pl.when(there)
+            def _():
+                action()
+
+    each(zip(has, [c.start for c in (rows_next, rows_prev, tile_next, tile_prev)]))
+    each([(has[1], rows_next.wait_recv), (has[0], rows_prev.wait_recv)])
+    each([(has[2], rim_next.start), (has[3], rim_prev.start)])
+    each([(has[3], tile_next.wait_recv), (has[2], tile_prev.wait_recv)])
+    each([(has[3], rim_next.wait_recv), (has[2], rim_prev.wait_recv)])
+    lane = lax.broadcasted_iota(jnp.int32, zt_ref.shape[1:], 1)
+
+    def merge(x, carry):
+        zt_ref[x] = jnp.where(lane < LANES // 2, right_ref[x], left_ref[x])
+        return carry
+
+    lax.fori_loop(0, zt_ref.shape[0], merge, 0)
+    each(zip(has, [c.wait_send for c in (rows_next, rows_prev, tile_next, tile_prev)]))
+    each([(has[2], rim_next.wait_send), (has[3], rim_prev.wait_send)])
 
 
 def update_kernel(count, sides, part_ref, old_ref, factor_ref, out_ref, held, send, recv, send2, recv2):
@@ -322,7 +397,6 @@
     height, depth = rows * count_y, cols * count_z
     modes_x, modes = velocity_modes.shape[1:3]
     tall, wide = rows + 2 * HALO, cols + LANES
-    index_y, index_z = lax.axis_index("ha"), lax.axis_index("dev")
 
     expand_y, expand_z, project_y, project_z = [], [], [], []
     for i in range(count_y):
@@ -342,11 +416,8 @@
             table[c, :, 1, c * modes : (c + 1) * modes] = low.T[:cols]
         project_z.append(table.reshape(3 * cols, 2 * LANES))
 
-    def pick(tables, index):
-        return lax.dynamic_index_in_dim(jnp.asarray(np.stack(tables)), index, 0, keepdims=False)
-
-    by_wide, by_back = pick(expand_y, index_y), pick(project_y, index_y)
-    bz_wide, bz_back = pick(expand_z, index_z), pick(project_z, index_z)
+    by_wide, by_back = jnp.asarray(np.stack(expand_y)), jnp.asarray(np.stack(project_y))
+    bz_wide, bz_back = jnp.asarray(np.stack(expand_z)), jnp.asarray(np.stack(project_z))
     bx = jnp.asarray(basis(np.arange(planes), planes, modes_x))
     factor = mode_factor((planes, height, depth), (modes_x, modes, modes))
     factor = np.tile(factor, (1, 1, LANES // modes)).astype(np.float32).reshape(-1, LANES)
@@ -395,9 +466,21 @@
         name="update",
     )
 
+    sheet = jax.ShapeDtypeStruct((planes, tall, LANES), F32)
+    halo = pl.pallas_call(
+        functools.partial(halo_kernel, count_y, count_z),
+        out_shape=(jax.ShapeDtypeStruct((planes, 2 * HALO, cols), F32), sheet),
+        in_specs=[VMEM],
+        out_specs=(VMEM, VMEM),
+        scratch_shapes=[pltpu.VMEM(sheet.shape, F32)] * 2 + [pltpu.SemaphoreType.DMA((6,))] * 2,
+        compiler_params=pltpu.CompilerParams(collective_id=1, has_side_effects=True),
+        name="halo",
+    )
+
     old = widen(velocity_modes.transpose(1, 2, 0, 3).reshape(modes_x, modes, 3 * modes))
-    adjoint_halo = halo_of(adjoint_field)
-    image_halo = halo_of(brain_image)
+    adjoint_halo = halo(adjoint_field)
+    image_source, adjoint_halo = lax.optimization_barrier((brain_image, adjoint_halo))
+    image_halo = halo_of(image_source)
     adjoint_end = transport(old, bx * -scale, by_wide, bz_wide, adjoint_field, *adjoint_halo)
     partial = project(adjoint_end, brain_image, *image_halo, bx, by_back, bz_back)
     updated = update(partial.reshape(entries, LANES), old.reshape(entries, LANES), factor)

time: 184 us -> 156 us (0.85)
  starting transfers between devices: 23 us -> 11.8 us
  local copies, waits for them, and re-layouts: 19.3 us -> 11.1 us
  Pallas kernels: 127 us -> 119 us
    pallas_call x0 -> x1, Pallas kernels: none -> 22.6 us  [per_device(): adjoint_halo = halo(adjoint_field)]
    pallas_call x1, Pallas kernels: 48.1 us -> 32.8 us  [per_device(): transport(updated, bx * scale, by_wide, bz_wide, brain_image, *image_halo)]
    pallas_call x1, Pallas kernels: 48 us -> 32.8 us  [per_device(): transport(old, bx * -scale, by_wide, bz_wide, adjoint_field, *adjoint_halo)]
    squeeze x4 -> x0, local copies, waits for them, and re-layouts: 6.11 us -> none  [pick(): lax.dynamic_index_in_dim(jnp.asarray(np.stack(tables)), index, 0, keepdim...]
    ppermute x2 -> x1, starting transfers between devices: 11.1 us -> 6.2 us  [halo_of(): before = lax.ppermute(field[:, -HALO:, :], 'ha', forward)]
    optimization_barrier x0 -> x1, local copies, waits for them, and re-layouts: none -> 4.16 us  [per_device(): lax.optimization_barrier((brain_image, adjoint_halo))]
    ppermute x2 -> x1, starting transfers between devices: 6.73 us -> 3.04 us  [halo_of(): left = lax.ppermute(tail, 'dev', forward)]
    slice x2 -> x1, local copies, waits for them, and re-layouts: 4.21 us -> 0.8 us  [halo_of(): before = lax.ppermute(field[:, -HALO:, :], 'ha', forward)]
  transfers between devices with their start and end apart: 8 -> 4, of which waited for: 2 -> 2; matrix products, arithmetic and copies ran while one was open for 8% -> 5% of each run, Pallas kernels for 0% -> 21%
where the time goes in v2:
time: 156 us
  Pallas kernels  119 us (76%)
  starting transfers between devices  11.8 us (8%)
  waiting for transfers between devices  11.4 us (7%)
  local copies, waits for them, and re-layouts  11.1 us (7%)
    pallas_call x1, Pallas kernels, per_device(): transport(old, bx * -scale, by_wide, bz_wide, adjoint_field, *adjoint_halo)  32.8 us
    pallas_call x1, Pallas kernels, per_device(): transport(updated, bx * scale, by_wide, bz_wide, brain_image, *image_halo)  32.8 us
    pallas_call x1, Pallas kernels, per_device(): adjoint_halo = halo(adjoint_field)  22.6 us
    pallas_call x1, Pallas kernels, per_device(): update(partial.reshape(entries, LANES), old.reshape(entries, LANES), factor)  19.1 us
    pallas_call x1, Pallas kernels, per_device(): project(adjoint_end, brain_image, *image_halo, bx, by_back, bz_back)  12.1 us
    ppermute x1, waiting for transfers between devices, halo_of(): before = lax.ppermute(field[:, -HALO:, :], 'ha', forward)  8.64 us
    ppermute x1, starting transfers between devices, halo_of(): before = lax.ppermute(field[:, -HALO:, :], 'ha', forward)  6.2 us
    optimization_barrier x1, local copies, waits for them, and re-layouts, per_device(): lax.optimization_barrier((brain_image, adjoint_halo))  4.16 us
  transfers between devices with their start and end apart: 4, of which 2 were waited for; matrix products, arithmetic and copies ran while one was open for 5% of the time, Pallas kernels for 21%

profile of v2, /device:TPU:0, one launch (start us, length us, event | category | flops | bytes accessed | tf_op | source)
XLA Modules:
  0.0 155.9 jit_solution(16349609114012919777)
XLA Ops:
  0.6 22.6 %halo.1 = (f32[32,16,384]{2,1,0:T(8,128)}, f32[32,48,128]{2,1,0:T(8,128)}) custom-call(f32[32,32,384]{2,1,0:T(8,128)} %q_ref.5), custom_call_target="tpu_custom_call" | custom-call | tf_op jit(solution)/shard_map/halo/pallas_call | solution.py:481
  23.3 0.8 fusion.1
  24.1 1.3 collective-permute-start
  25.4 6.2 %collective-permute-start.1 = (f32[32,8,384]{2,1,0:T(8,128)}, f32[32,8,384]{2,1,0:T(8,128)S(1)}, u32[]{:S(2)}, u32[]{:S(2)}) collective-permute-start(f32[32,8,384]{2,1,0:T(8,128)} %get-tuple-element.21), channel_id=1, source_target_pairs={{0,2},{2,4},{4,6},{6,8},{8,10},{10,12},{12,14},{1,3},{3,5},{5,7},{... | collective-permute-start | bytes 1179656 | tf_op jit(solution)/shard_map/ppermute | solution.py:379
  31.6 4.2 %copy.17 = f32[32,32,384]{1,2,0:T(8,128)} copy(f32[32,32,384]{2,1,0:T(8,128)S(1)} %copy-done) | data formatting | bytes 3145728 | tf_op jit(solution)/shard_map/optimization_barrier | solution.py:482
  35.7 1.0 fusion
  36.7 2.7 %collective-permute-done = f32[32,8,384]{2,1,0:T(8,128)S(1)} collective-permute-done((f32[32,8,384]{2,1,0:T(8,128)S(1)}, f32[32,8,384]{2,1,0:T(8,128)S(1)}, u32[]{:S(2)}, u32[]{:S(2)}) %collective-permute-start) | collective-permute-done | bytes 393248 | tf_op jit(solution)/shard_map/ppermute | solution.py:380
  39.5 8.6 %collective-permute-done.1 = f32[32,8,384]{2,1,0:T(8,128)S(1)} collective-permute-done((f32[32,8,384]{2,1,0:T(8,128)}, f32[32,8,384]{2,1,0:T(8,128)S(1)}, u32[]{:S(2)}, u32[]{:S(2)}) %collective-permute-start.1) | collective-permute-done | bytes 393248 | tf_op jit(solution)/shard_map/ppermute | solution.py:379
  48.1 0.1 fusion.2
  48.4 0.1 pad_maximum_fusion.1
  48.5 1.3 collective-permute-start.2
  50.1 3.0 %collective-permute-start.3 = (f32[32,48,8]{1,2,0:T(8,128)S(1)}, f32[32,48,8]{1,2,0:T(8,128)S(1)}, u32[]{:S(2)}, u32[]{:S(2)}) collective-permute-start(f32[32,48,8]{1,2,0:T(8,128)S(1)} %pad_maximum_fusion.2), channel_id=1, source_target_pairs={{0,1},{2,3},{4,5},{6,7},{8,9},{10,11},{12,13},{14,15},{16,17},{18,... | collective-permute-start | bytes 147464 | tf_op jit(solution)/shard_map/ppermute | solution.py:387
  53.1 0.5 copy.16
  53.7 0.4 reshape.21
  54.1 0.7 pad.4.v_ref
  54.9 32.8 %transport.2.adj_ref = f32[32,32,384]{2,1,0:T(8,128)} custom-call(f32[16,32,128]{2,1,0:T(8,128)} %pad.4.v_ref, f32[32,16]{1,0:T(8,128)} %constant.29.bx_ref, bf16[8,48,96]{2,1,0:T(8,128)(2,1)} %constant.20.clone.by_ref, bf16[2,128,512]{2,1,0:T(8,128)(2,1)} %constant.22.clone.bz_ref, f32[32,32,384]{2,1,0:T(8,128)} %q_ref.5, ...), custom_call_target="tpu_custom_call" | custom-call | flops 157286400 | bytes 60000000 | tf_op jit(solution)/shard_map/transport/pallas_call | solution.py:484
  87.7 0.3 copy.21
  88.0 0.3 copy.22
  88.3 1.2 pad_maximum_fusion.zt_ref
  89.5 12.1 %project.1 = f32[16,32,128]{2,1,0:T(8,128)} custom-call(f32[32,32,384]{2,1,0:T(8,128)} %transport.2.adj_ref, f32[32,32,384]{2,1,0:T(8,128)} %q_ref.7, f32[32,16,384]{2,1,0:T(8,128)} %copy-done.1, f32[32,48,128]{2,1,0:T(8,128)} %pad_maximum_fusion.zt_ref, f32[32,16]{1,0:T(8,128)} %constant.24.clone.bx_ref, bf16[8,32,96]{2,1,0:T(8,128)(2,1)} %constant.21.clone.by_ref, ...), custom_call_target="tpu_custom_call" | custom-call | tf_op jit(solution)/shard_map/project/pallas_call | solution.py:485
  101.5 19.1 %update.1 = f32[512,128]{1,0:T(8,128)} custom-call(f32[512,128]{1,0:T(8,128)} %bitcast.10, f32[512,128]{1,0:T(8,128)} %bitcast.7, f32[512,128]{1,0:T(8,128)} %constant.25.clone.factor_ref), custom_call_target="tpu_custom_call" | custom-call | tf_op jit(solution)/shard_map/update/pallas_call | solution.py:486
  120.6 1.5 reshape.25
  122.1 1.0 copy.23
  123.1 32.8 %transport.3 = f32[32,32,384]{2,1,0:T(8,128)} custom-call(f32[16,32,128]{2,1,0:T(8,128)} %bitcast.9, f32[32,16]{1,0:T(8,128)} %constant.30.bx_ref, bf16[8,48,96]{2,1,0:T(8,128)(2,1)} %constant.20.clone.by_ref, bf16[2,128,512]{2,1,0:T(8,128)(2,1)} %constant.22.clone.bz_ref, f32[32,32,384]{2,1,0:T(8,128)} %q_ref.7, f32[32,16,384]{2,1,0:T(8,128)} %copy-done.1, ...), custom_call_target="tpu_custom_call" | custom-call | flops 157286400 | bytes 60000000 | tf_op jit(solution)/shard_map/transport/pallas_call | solution.py:488
  (15 shorter events, 0.5 us)
Async XLA Ops:
  0.6 22.6 %copy-start = (f32[32,32,384]{2,1,0:T(8,128)S(1)}, f32[32,32,384]{2,1,0:T(8,128)}, u32[]{:S(2)}) copy-start(f32[32,32,384]{2,1,0:T(8,128)} %q_ref.7) | copy-start | bytes 4718596
  24.1 15.4 %collective-permute-start = (f32[32,8,384]{2,1,0:T(8,128)S(1)}, f32[32,8,384]{2,1,0:T(8,128)S(1)}, u32[]{:S(2)}, u32[]{:S(2)}) collective-permute-start(f32[32,8,384]{2,1,0:T(8,128)S(1)} %get-tuple-element.22), channel_id=1, source_target_pairs={{2,0},{4,2},{6,4},{8,6},{10,8},{12,10},{14,12},{3,1},{5,3},{7,5},{... | collective-permute-start | bytes 1179656 | tf_op jit(solution)/shard_map/ppermute | solution.py:380
  25.4 22.7 %collective-permute-start.1 = (f32[32,8,384]{2,1,0:T(8,128)}, f32[32,8,384]{2,1,0:T(8,128)S(1)}, u32[]{:S(2)}, u32[]{:S(2)}) collective-permute-start(f32[32,8,384]{2,1,0:T(8,128)} %get-tuple-element.21), channel_id=1, source_target_pairs={{0,2},{2,4},{4,6},{6,8},{8,10},{10,12},{12,14},{1,3},{3,5},{5,7},{... | collective-permute-start | bytes 1179656 | tf_op jit(solution)/shard_map/ppermute | solution.py:379
  39.4 13.7 %copy-start.2 = (f32[3,16,32,32]{3,2,1,0:T(8,128)S(1)}, f32[3,16,32,32]{3,2,1,0:T(8,128)}, u32[]{:S(2)}) copy-start(f32[3,16,32,32]{3,2,1,0:T(8,128)} %param.11) | copy-start | bytes 589828
  48.1 5.5 %copy-start.1 = (f32[32,16,384]{2,1,0:T(8,128)}, f32[32,16,384]{2,1,0:T(8,128)S(1)}, u32[]{:S(2)}) copy-start(f32[32,16,384]{2,1,0:T(8,128)S(1)} %constant_dynamic-update-slice_fusion.yh_ref) | copy-start | bytes 2359300
  48.5 39.1 %collective-permute-start.2 = (f32[32,48,8]{1,2,0:T(8,128)S(1)}, f32[32,48,8]{1,2,0:T(8,128)S(1)}, u32[]{:S(2)}, u32[]{:S(2)}) collective-permute-start(f32[32,48,8]{1,2,0:T(8,128)S(1)} %pad_maximum_fusion.1), channel_id=1, source_target_pairs={{1,0},{3,2},{5,4},{7,6},{9,8},{11,10},{13,12},{15,14},{17,16},{19,... | collective-permute-start | bytes 147464 | tf_op jit(solution)/shard_map/ppermute | solution.py:388
  50.1 37.9 %collective-permute-start.3 = (f32[32,48,8]{1,2,0:T(8,128)S(1)}, f32[32,48,8]{1,2,0:T(8,128)S(1)}, u32[]{:S(2)}, u32[]{:S(2)}) collective-permute-start(f32[32,48,8]{1,2,0:T(8,128)S(1)} %pad_maximum_fusion.2), channel_id=1, source_target_pairs={{0,1},{2,3},{4,5},{6,7},{8,9},{10,11},{12,13},{14,15},{16,17},{18,... | collective-permute-start | bytes 147464 | tf_op jit(solution)/shard_map/ppermute | solution.py:387

commit v3 on v1

--- a/solution.py
+++ b/solution.py
@@ -63,6 +63,7 @@
 
 def expand_kernel(planes, modes_x, modes, v_ref, bx_ref, by_ref, bz_ref, coefs):
     height, depth = coefs[0].shape[1:]
+    by, bz = by_ref[lax.axis_index("ha")], bz_ref.at[lax.axis_index("dev")]
     group = lax.broadcasted_iota(jnp.int32, (height, LANES), 1) // modes
 
     def body(x, carry):
@@ -71,7 +72,7 @@
             weighted = weighted + bx_ref[x, a] * v_ref[a]
         high, low = split(weighted)
         rows = jnp.concatenate([high, low, high], axis=0)
-        mixed = jnp.dot(by_ref[...], rows, preferred_element_type=F32)
+        mixed = jnp.dot(by, rows, preferred_element_type=F32)
         top = mixed.astype(BF16).astype(F32)
         rest = mixed - top
         total = jnp.ones((height, depth), F32)
@@ -80,7 +81,7 @@
             second = pltpu.roll(top, ((1 - c) * modes) % LANES, 1) if c != 1 else top
             third = pltpu.roll(rest, ((2 - c) * modes) % LANES, 1) if c != 2 else rest
             left = jnp.where(group == 0, first, jnp.where(group == 1, second, third))
-            speed = jnp.dot(left.astype(BF16), bz_ref[...], preferred_element_type=F32)
+            speed = jnp.dot(left.astype(BF16), bz[...], preferred_element_type=F32)
             plus = jnp.maximum(speed, 0.0)
             minus = jnp.maximum(-speed, 0.0)
             coefs[1 + 2 * c][x] = plus
@@ -89,10 +90,10 @@
         coefs[0][x] = total
         return carry
 
-    lax.fori_loop(0, planes, body, 0)
-
-
-def gather_field(q_ref, yh_ref, zt_ref, field):
+    lax.fori_loop(0, planes, body, 0, unroll=2)
+
+
+def gather_field(q_ref, yh_ref, tile, field):
     planes, rows, depth = q_ref.shape
     height = field.shape[1]
     field[0] = jnp.zeros(field.shape[1:], F32)
@@ -101,7 +102,7 @@
     def body(x, carry):
         field[x + 1, 0:rows, 0:depth] = q_ref[x]
         field[x + 1, rows:height, 0:depth] = yh_ref[x]
-        field[x + 1, :, depth : depth + LANES] = zt_ref[x]
+        field[x + 1, :, depth : depth + LANES] = tile(x)
         return carry
 
     lax.fori_loop(0, planes, body, 0)
@@ -152,17 +153,9 @@
     return results
 
 
-def transport_kernel(
-    planes, modes_x, modes, v_ref, bx_ref, by_ref, bz_ref, q_ref, yh_ref, zt_ref, out_ref, *scratch
-):
-    field, middle = scratch[:2]
-    coefs = scratch[2:]
+def transport(planes, q_ref, out_ref, field, middle, coefs, between):
     height, width = field.shape[1:]
     rows, depth = q_ref.shape[1:]
-    gather_field(q_ref, yh_ref, zt_ref, field)
-    middle[0] = jnp.zeros((height, width), F32)
-    middle[planes + 1] = jnp.zeros((height, width), F32)
-    expand_kernel(planes, modes_x, modes, v_ref, bx_ref, by_ref, bz_ref, coefs)
 
     def first(x, carry):
         for t, value in enumerate(stencil(field, x, coefs, height, width)):
@@ -182,13 +175,59 @@
         return carry
 
     def step(i, carry):
-        lax.fori_loop(0, planes, first, 0)
-        lax.fori_loop(0, planes, second, 0)
+        lax.fori_loop(0, planes, first, 0, unroll=4)
+        lax.fori_loop(0, planes, second, 0, unroll=4)
         return carry
 
     lax.fori_loop(0, STEPS - 1, step, 0)
-    lax.fori_loop(0, planes, first, 0)
-    lax.fori_loop(0, planes, last, 0)
+    between()
+    lax.fori_loop(0, planes, first, 0, unroll=4)
+    lax.fori_loop(0, planes, last, 0, unroll=4)
+
+
+def adjoint_kernel(
+    planes, modes_x, modes, count_y, count_z, v_ref, bx_ref, by_ref, bz_ref, q_ref, image_ref,
+    out_ref, image_yh, image_zt, yh_ref, left, right, image_left, image_right,
+    send, recv, image_send, image_recv, field, middle, *coefs
+):
+    has, peers = neighbours(count_y, count_z)
+    mine = Exchange(has, peers, q_ref, yh_ref, left, right, send, recv)
+    image = Exchange(
+        has, peers, image_ref, image_yh, image_left, image_right, image_send, image_recv
+    )
+    mine.clear()
+    image.clear()
+    greet(has, peers)
+    mine.start()
+    middle[0] = jnp.zeros(middle.shape[1:], F32)
+    middle[planes + 1] = jnp.zeros(middle.shape[1:], F32)
+    expand_kernel(planes, modes_x, modes, v_ref, bx_ref, by_ref, bz_ref, coefs)
+    mine.forward()
+    image.start()
+    mine.finish()
+    gather_field(q_ref, yh_ref, mine.tile, field)
+    transport(planes, q_ref, out_ref, field, middle, coefs, image.forward)
+    image.finish()
+
+    def merge(x, carry):
+        image_zt[x] = image.tile(x)
+        return carry
+
+    lax.fori_loop(0, planes, merge, 0)
+
+
+def image_kernel(
+    planes, modes_x, modes, v_ref, bx_ref, by_ref, bz_ref, q_ref, yh_ref, zt_ref,
+    out_ref, next_ref, field, middle, *coefs
+):
+    for c in range(3):
+        for a in range(modes_x):
+            next_ref[c, a] = v_ref[a][:, c * modes : (c + 1) * modes]
+    middle[0] = jnp.zeros(middle.shape[1:], F32)
+    middle[planes + 1] = jnp.zeros(middle.shape[1:], F32)
+    gather_field(q_ref, yh_ref, lambda x: zt_ref[x], field)
+    expand_kernel(planes, modes_x, modes, v_ref, bx_ref, by_ref, bz_ref, coefs)
+    transport(planes, q_ref, out_ref, field, middle, coefs, lambda: None)
 
 
 def project_kernel(
@@ -196,7 +235,8 @@
 ):
     height, width = field.shape[1:]
     rows, depth = q_ref.shape[1:]
-    gather_field(q_ref, yh_ref, zt_ref, field)
+    gather_field(q_ref, yh_ref, lambda x: zt_ref[x], field)
+    by, bz = by_ref[lax.axis_index("ha")], bz_ref.at[lax.axis_index("dev")]
 
     def body(x, carry):
         plane = field[x + 1]
@@ -219,7 +259,7 @@
     def multiply(i, carry):
         start = i * (chunk * 2 * rows)
         wide = jnp.dot(
-            forcing[pl.ds(start, chunk * 2 * rows), :], bz_ref[...], preferred_element_type=F32
+            forcing[pl.ds(start, chunk * 2 * rows), :], bz[...], preferred_element_type=F32
         )
         wide = wide[:, 0:LANES] + wide[:, LANES : 2 * LANES]
         wide = wide.reshape(chunk, 2 * rows, LANES)
@@ -234,7 +274,7 @@
             total = total + bx_ref[x, a] * inner[x]
         high, low = split(total)
         stacked = jnp.concatenate([high, low, high], axis=0)
-        out_ref[a] = jnp.dot(by_ref[...], stacked, preferred_element_type=F32)
+        out_ref[a] = jnp.dot(by, stacked, preferred_element_type=F32)
         return carry
 
     lax.fori_loop(0, modes_x, finish, 0)
@@ -242,6 +282,95 @@
 
 def peer_of(index, sides):
     return {"ha": index // sides, "dev": lax.rem(index, sides)}
+
+
+MESH = pl.DeviceIdType.MESH
+
+
+def neighbours(count_y, count_z):
+    me_y, me_z = lax.axis_index("ha"), lax.axis_index("dev")
+    has = (me_y < count_y - 1, me_y > 0, me_z < count_z - 1, me_z > 0)
+    peers = ({"ha": me_y + 1}, {"ha": me_y - 1}, {"dev": me_z + 1}, {"dev": me_z - 1})
+    return has, peers
+
+
+def each(pairs):
+    for there, action in pairs:
+
+        @pl.when(there)
+        def _():
+            action()
+
+
+def greet(has, peers):
+    barrier = pltpu.get_barrier_semaphore()
+    for there, peer in zip(has, peers):
+
+        @pl.when(there)
+        def _():
+            pl.semaphore_signal(barrier, inc=1, device_id=peer, device_id_type=MESH)
+
+    pl.semaphore_wait(barrier, sum(jnp.where(there, 1, 0) for there in has))
+
+
+class Exchange:
+    def __init__(self, has, peers, q_ref, yh_ref, left_ref, right_ref, send, recv):
+        rows, cols = q_ref.shape[1:]
+        last = slice(cols - LANES, cols)
+        first = slice(0, LANES)
+        before, after = slice(HALO, 2 * HALO), slice(0, HALO)
+        block, rim = slice(0, rows), slice(rows, rows + 2 * HALO)
+
+        def copy(source, target, slot, peer):
+            return pltpu.make_async_remote_copy(
+                src_ref=source,
+                dst_ref=target,
+                send_sem=send.at[slot],
+                recv_sem=recv.at[slot],
+                device_id=peer,
+                device_id_type=MESH,
+            )
+
+        self.has = has
+        self.sides = left_ref, right_ref
+        self.targets = yh_ref.at[:, after], yh_ref.at[:, before], right_ref, left_ref
+        self.blocks = (
+            copy(q_ref.at[:, rows - HALO : rows], yh_ref.at[:, before], 0, peers[0]),
+            copy(q_ref.at[:, 0:HALO], yh_ref.at[:, after], 1, peers[1]),
+            copy(q_ref.at[:, :, last], left_ref.at[:, block], 2, peers[2]),
+            copy(q_ref.at[:, :, first], right_ref.at[:, block], 3, peers[3]),
+        )
+        self.rims = (
+            copy(yh_ref.at[:, :, last], left_ref.at[:, rim], 4, peers[2]),
+            copy(yh_ref.at[:, :, first], right_ref.at[:, rim], 5, peers[3]),
+        )
+
+    def clear(self):
+        for there, target in zip(self.has, self.targets):
+
+            @pl.when(jnp.logical_not(there))
+            def _():
+                target[...] = jnp.zeros(target.shape, F32)
+
+    def start(self):
+        each(zip(self.has, [copy.start for copy in self.blocks]))
+
+    def forward(self):
+        up, down, right, left = self.has
+        each([(down, self.blocks[0].wait_recv), (up, self.blocks[1].wait_recv)])
+        each([(right, self.rims[0].start), (left, self.rims[1].start)])
+
+    def finish(self):
+        up, down, right, left = self.has
+        each([(left, self.blocks[2].wait_recv), (right, self.blocks[3].wait_recv)])
+        each([(left, self.rims[0].wait_recv), (right, self.rims[1].wait_recv)])
+        each(zip(self.has, [copy.wait_send for copy in self.blocks]))
+        each([(right, self.rims[0].wait_send), (left, self.rims[1].wait_send)])
+
+    def tile(self, x):
+        left_ref, right_ref = self.sides
+        lane = lax.broadcasted_iota(jnp.int32, left_ref.shape[1:], 1)
+        return jnp.where(lane < LANES // 2, right_ref[x], left_ref[x])
 
 
 def update_kernel(count, sides, part_ref, old_ref, factor_ref, out_ref, held, send, recv, send2, recv2):
@@ -297,24 +426,6 @@
 PARAMS = pltpu.CompilerParams(vmem_limit_bytes=60 * 1024 * 1024)
 
 
-def halo_of(field):
-    count = lax.axis_size("ha")
-    forward = [(i, i + 1) for i in range(count - 1)]
-    backward = [(i + 1, i) for i in range(count - 1)]
-    before = lax.ppermute(field[:, -HALO:, :], "ha", forward)
-    after = lax.ppermute(field[:, :HALO, :], "ha", backward)
-    sides = lax.axis_size("dev")
-    forward = [(i, i + 1) for i in range(sides - 1)]
-    backward = [(i + 1, i) for i in range(sides - 1)]
-    rows = jnp.concatenate([after, before], axis=1)
-    head = jnp.concatenate([field[:, :, :HALO], rows[:, :, :HALO]], axis=1)
-    tail = jnp.concatenate([field[:, :, -HALO:], rows[:, :, -HALO:]], axis=1)
-    left = lax.ppermute(tail, "dev", forward)
-    right = lax.ppermute(head, "dev", backward)
-    gap = jnp.zeros(left.shape[:2] + (LANES - 2 * HALO,), F32)
-    return rows, jnp.concatenate([right, gap, left], axis=2)
-
-
 def per_device(brain_image, adjoint_field, velocity_modes):
     planes, rows, cols = brain_image.shape
     count_y = lax.axis_size("ha")
@@ -322,7 +433,6 @@
     height, depth = rows * count_y, cols * count_z
     modes_x, modes = velocity_modes.shape[1:3]
     tall, wide = rows + 2 * HALO, cols + LANES
-    index_y, index_z = lax.axis_index("ha"), lax.axis_index("dev")
 
     expand_y, expand_z, project_y, project_z = [], [], [], []
     for i in range(count_y):
@@ -342,11 +452,8 @@
             table[c, :, 1, c * modes : (c + 1) * modes] = low.T[:cols]
         project_z.append(table.reshape(3 * cols, 2 * LANES))
 
-    def pick(tables, index):
-        return lax.dynamic_index_in_dim(jnp.asarray(np.stack(tables)), index, 0, keepdims=False)
-
-    by_wide, by_back = pick(expand_y, index_y), pick(project_y, index_y)
-    bz_wide, bz_back = pick(expand_z, index_z), pick(project_z, index_z)
+    by_wide, by_back = jnp.asarray(np.stack(expand_y)), jnp.asarray(np.stack(project_y))
+    bz_wide, bz_back = jnp.asarray(np.stack(expand_z)), jnp.asarray(np.stack(project_z))
     bx = jnp.asarray(basis(np.arange(planes), planes, modes_x))
     factor = mode_factor((planes, height, depth), (modes_x, modes, modes))
     factor = np.tile(factor, (1, 1, LANES // modes)).astype(np.float32).reshape(-1, LANES)
@@ -356,17 +463,32 @@
         return jnp.pad(value, ((0, 0), (0, 0), (0, LANES - 3 * modes)))
 
     plane = pltpu.VMEM((planes + 2, tall, wide), F32)
-    transport = pl.pallas_call(
-        functools.partial(transport_kernel, planes, modes_x, modes),
-        out_shape=jax.ShapeDtypeStruct((planes, rows, cols), F32),
+    block = jax.ShapeDtypeStruct((planes, rows, cols), F32)
+    rims = jax.ShapeDtypeStruct((planes, 2 * HALO, cols), F32)
+    sheet = jax.ShapeDtypeStruct((planes, tall, LANES), F32)
+    work = [plane, plane] + [pltpu.VMEM((planes, tall, wide), F32)] * 7
+    adjoint_transport = pl.pallas_call(
+        functools.partial(adjoint_kernel, planes, modes_x, modes, count_y, count_z),
+        out_shape=(block, rims, sheet),
+        in_specs=[VMEM, SMEM, VMEM, VMEM, VMEM, VMEM],
+        out_specs=(VMEM, VMEM, VMEM),
+        scratch_shapes=[pltpu.VMEM(rims.shape, F32)]
+        + [pltpu.VMEM(sheet.shape, F32)] * 4
+        + [pltpu.SemaphoreType.DMA((6,))] * 4
+        + work,
+        compiler_params=pltpu.CompilerParams(
+            vmem_limit_bytes=60 * 1024 * 1024, collective_id=1, has_side_effects=True
+        ),
+        name="adjoint_transport",
+    )
+    image_transport = pl.pallas_call(
+        functools.partial(image_kernel, planes, modes_x, modes),
+        out_shape=(block, jax.ShapeDtypeStruct(velocity_modes.shape, F32)),
         in_specs=[VMEM, SMEM, VMEM, VMEM, VMEM, VMEM, VMEM],
-        out_specs=VMEM,
-        scratch_shapes=[plane, plane] + [pltpu.VMEM((planes, tall, wide), F32)] * 7,
+        out_specs=(VMEM, VMEM),
+        scratch_shapes=work,
         compiler_params=PARAMS,
-        cost_estimate=pl.CostEstimate(
-            flops=200 * planes * tall * wide, bytes_accessed=60_000_000, transcendentals=0
-        ),
-        name="transport",
+        name="image_transport",
     )
     project = pl.pallas_call(
         functools.partial(project_kernel, planes, modes_x),
@@ -396,15 +518,19 @@
     )
 
     old = widen(velocity_modes.transpose(1, 2, 0, 3).reshape(modes_x, modes, 3 * modes))
-    adjoint_halo = halo_of(adjoint_field)
-    image_halo = halo_of(brain_image)
-    adjoint_end = transport(old, bx * -scale, by_wide, bz_wide, adjoint_field, *adjoint_halo)
+    adjoint_end, *image_halo = adjoint_transport(
+        old, bx * -scale, by_wide, bz_wide, adjoint_field, brain_image
+    )
     partial = project(adjoint_end, brain_image, *image_halo, bx, by_back, bz_back)
     updated = update(partial.reshape(entries, LANES), old.reshape(entries, LANES), factor)
-    updated = updated.reshape(modes_x, modes, LANES)
-    image_end = transport(updated, bx * scale, by_wide, bz_wide, brain_image, *image_halo)
-    velocity_next = updated[:, :, : 3 * modes].reshape(modes_x, modes, 3, modes)
-    velocity_next = velocity_next.transpose(2, 0, 1, 3)
+    image_end, velocity_next = image_transport(
+        updated.reshape(modes_x, modes, LANES),
+        bx * scale,
+        by_wide,
+        bz_wide,
+        brain_image,
+        *image_halo,
+    )
     return (adjoint_end, image_end, velocity_next)
 
 

time: 184 us -> 116 us (0.63)
  starting transfers between devices: 23 us -> 0 us
  local copies, waits for them, and re-layouts: 19.3 us -> 3.95 us
  Pallas kernels: 127 us -> 112 us
  waiting for transfers between devices: 11 us -> 0 us
  other arithmetic: 2.11 us -> 0 us
    ppermute x8 -> x0, starting transfers between devices: 23 us -> none  [the longest x2 11.1 us: halo_of(): before = lax.ppermute(field[:, -HALO:, :], 'ha', forward)]
    pallas_call x2, Pallas kernels: 96.1 us -> 77.3 us  [the longest x1 44.1 us: per_device(): adjoint_transport(old, bx * -scale, by_wide, bz_wide, adjoint_field, brai...]
    ppermute x8 -> x0, waiting for transfers between devices: 11 us -> none  [the longest x2 11 us: halo_of(): before = lax.ppermute(field[:, -HALO:, :], 'ha', forward)]
    squeeze x4 -> x0, local copies, waits for them, and re-layouts: 6.11 us -> none  [pick(): lax.dynamic_index_in_dim(jnp.asarray(np.stack(tables)), index, 0, keepdim...]
    slice x10 -> x0, local copies, waits for them, and re-layouts: 6.1 us -> none  [the longest x2 4.21 us: halo_of(): before = lax.ppermute(field[:, -HALO:, :], 'ha', forward)]
    pallas_call x1, Pallas kernels: 19.1 us -> 22.3 us  [per_device(): update(partial.reshape(entries, LANES), old.reshape(entries, LANES), factor)]
    concatenate x5 -> x0, other arithmetic: 2.11 us -> none  [the longest x1 1.62 us: halo_of(): return (rows, jnp.concatenate([right, gap, left], axis=2))]
    ppermute x4 -> x0, local copies, waits for them, and re-layouts: 2.03 us -> none  [the longest x2 1.47 us: halo_of(): left = lax.ppermute(tail, 'dev', forward)]
  transfers between devices with their start and end apart: 8 -> 0, of which waited for: 2 -> 0; matrix products, arithmetic and copies ran while one was open for 8% -> 0% of each run, Pallas kernels for 0% -> 0%
where the time goes in v3:
time: 116 us
  Pallas kernels  112 us (97%)
  local copies, waits for them, and re-layouts  3.95 us (3%)
    pallas_call x1, Pallas kernels, per_device(): adjoint_transport(old, bx * -scale, by_wide, bz_wide, adjoint_field, brai...  44.1 us
    pallas_call x1, Pallas kernels, per_device(): image_transport(updated.reshape(modes_x, modes, LANES), bx * scale, by_wi...  33.1 us
    pallas_call x1, Pallas kernels, per_device(): update(partial.reshape(entries, LANES), old.reshape(entries, LANES), factor)  22.3 us
    pallas_call x1, Pallas kernels, per_device(): project(adjoint_end, brain_image, *image_halo, bx, by_back, bz_back)  12.1 us

profile of v3, /device:TPU:0, one launch (start us, length us, event | category | flops | bytes accessed | tf_op | source)
XLA Modules:
  0.0 116.3 jit_solution(11303270629544001490)
XLA Ops:
  0.6 1.7 %copy.13 = f32[16,32,3,32]{3,2,1,0:T(4,128)S(1)} copy(f32[16,32,3,32]{3,1,0,2:T(8,128)} %bitcast.7) | data formatting | bytes 393216 | tf_op jit(solution)/shard_map/transpose | solution.py:520
  2.3 0.4 reshape.18
  2.7 0.7 pad.4.v_ref
  3.4 44.1 %adjoint_transport.1 = (f32[32,32,384]{2,1,0:T(8,128)}, f32[32,16,384]{2,1,0:T(8,128)}, f32[32,48,128]{2,1,0:T(8,128)}) custom-call(f32[16,32,128]{2,1,0:T(8,128)} %pad.4.v_ref, f32[32,16]{1,0:T(8,128)} %constant.28.bx_ref, bf16[8,48,96]{2,1,0:T(8,128)(2,1)} %constant.19.clone.by_ref, bf16[2,128,512]{2,1,0:T(8,128)(2,1)} %constant.21.clone.bz_ref, ...), custom_call_target="tpu_custom_call" | custom-call | tf_op jit(solution)/shard_map/adjoint_transport/pallas_call | solution.py:521
  47.6 12.1 %project.1 = f32[16,32,128]{2,1,0:T(8,128)} custom-call(f32[32,32,384]{2,1,0:T(8,128)} %get-tuple-element.16.adj_ref, f32[32,32,384]{2,1,0:T(8,128)} %q_ref.5, f32[32,16,384]{2,1,0:T(8,128)} %get-tuple-element.9.yh_ref, f32[32,48,128]{2,1,0:T(8,128)} %get-tuple-element.10.zt_ref, f32[32,16]{1,0:T(8,128)} %constant.23.clone.bx_ref, ...), custom_call_target="tpu_custom_call" | custom-call | tf_op jit(solution)/shard_map/project/pallas_call | solution.py:524
  59.7 22.3 %update.1 = f32[512,128]{1,0:T(8,128)} custom-call(f32[512,128]{1,0:T(8,128)} %bitcast.5, f32[512,128]{1,0:T(8,128)} %bitcast.4, f32[512,128]{1,0:T(8,128)} %constant.24.clone.factor_ref), custom_call_target="tpu_custom_call" | custom-call | tf_op jit(solution)/shard_map/update/pallas_call | solution.py:525
  82.0 0.0 copy-start
  82.0 33.1 %image_transport.1 = (f32[32,32,384]{2,1,0:T(8,128)}, f32[3,16,32,32]{3,2,1,0:T(8,128)}) custom-call(f32[16,32,128]{2,1,0:T(8,128)} %bitcast.6, f32[32,16]{1,0:T(8,128)} %constant.29.bx_ref, bf16[8,48,96]{2,1,0:T(8,128)(2,1)} %constant.19.clone.by_ref, bf16[2,128,512]{2,1,0:T(8,128)(2,1)} %constant.21.clone.bz_ref, f32[32,32,384]{2,1,0:T(8,128)} %q_ref.5, ...), custom_call_target="tpu_custom_call" | custom-call | tf_op jit(solution)/shard_map/image_transport/pallas_call | solution.py:526
  115.1 0.0 copy-done
  115.1 1.1 copy.15
Async XLA Ops:
  82.0 33.1 %copy-start = (f32[32,32,384]{2,1,0:T(8,128)S(1)}, f32[32,32,384]{2,1,0:T(8,128)}, u32[]{:S(2)}) copy-start(f32[32,32,384]{2,1,0:T(8,128)} %get-tuple-element.16.adj_ref) | copy-start | bytes 4718596

commit v4 on v3

--- a/solution.py
+++ b/solution.py
@@ -94,95 +94,119 @@
 
 
 def gather_field(q_ref, yh_ref, tile, field):
+    tiles, height = field.shape[0], field.shape[2]
     planes, rows, depth = q_ref.shape
-    height = field.shape[1]
-    field[0] = jnp.zeros(field.shape[1:], F32)
-    field[planes + 1] = jnp.zeros(field.shape[1:], F32)
+    edge = jnp.zeros((height, LANES), F32)
+    spare = jnp.zeros((HALO, LANES), F32)
+    block = slice(2 * HALO, 2 * HALO + rows)
+    after = slice(2 * HALO + rows, 3 * HALO + rows)
+    before = slice(HALO, 2 * HALO)
+    for t in range(tiles):
+        field[t, 0] = edge
+        field[t, planes + 1] = edge
 
     def body(x, carry):
-        field[x + 1, 0:rows, 0:depth] = q_ref[x]
-        field[x + 1, rows:height, 0:depth] = yh_ref[x]
-        field[x + 1, :, depth : depth + LANES] = tile(x)
+        side = tile(x)
+        for t in range(tiles):
+            lanes = slice(t * LANES, (t + 1) * LANES)
+            field[t, x + 1, 0:HALO] = spare
+            field[t, x + 1, height - HALO : height] = spare
+            last = t == tiles - 1
+            field[t, x + 1, block] = side[0:rows] if last else q_ref[x, :, lanes]
+            field[t, x + 1, after] = (
+                side[rows : rows + HALO] if last else yh_ref[x, 0:HALO, lanes]
+            )
+            field[t, x + 1, before] = (
+                side[rows + HALO :] if last else yh_ref[x, HALO : 2 * HALO, lanes]
+            )
         return carry
 
     lax.fori_loop(0, planes, body, 0)
 
 
-def stencil(src, x, coefs, rows, depth):
-    height, width = src.shape[1:]
-    strips = height // 8
-    wanted = rows // 8
-    row = lax.broadcasted_iota(jnp.int32, (8, depth), 0)
-    tiles = {}
-    ups = {}
-    downs = {}
-
-    def tile(t):
-        t = t % strips
-        if t not in tiles:
-            tiles[t] = src[x + 1, 8 * t : 8 * t + 8, :]
-        return tiles[t]
-
-    def up(t):
-        t = t % strips
-        if t not in ups:
-            ups[t] = pltpu.roll(tile(t)[:, :depth], 1, 0)
-        return ups[t]
-
-    def down(t):
-        t = t % strips
-        if t not in downs:
-            downs[t] = pltpu.roll(tile(t)[:, :depth], 7, 0)
-        return downs[t]
-
-    results = []
-    for t in range(wanted):
-        part = pl.ds(8 * t, 8)
-
-        def coef(index):
-            return coefs[index][x, part, 0:depth]
-
-        q = tile(t)
-        total = coef(0) * q[:, :depth]
-        total = total + coef(1) * src[x, part, 0:depth] + coef(2) * src[x + 2, part, 0:depth]
-        total = total + coef(3) * jnp.where(row == 0, up(t - 1), up(t))
-        total = total + coef(4) * jnp.where(row == 7, down(t + 1), down(t))
-        total = total + coef(5) * pltpu.roll(q, 1, 1)[:, :depth]
-        total = total + coef(6) * pltpu.roll(q, width - 1, 1)[:, :depth]
-        results.append(total)
-    return results
+def clear_edges(middle):
+    tiles, planes, height = middle.shape[:3]
+    edge = jnp.zeros((height, LANES), F32)
+    spare = jnp.zeros((HALO, LANES), F32)
+    for t in range(tiles):
+        middle[t, 0] = edge
+        middle[t, planes - 1] = edge
+
+    def body(x, carry):
+        for t in range(tiles):
+            middle[t, x, 0:HALO] = spare
+            middle[t, x, height - HALO : height] = spare
+        return carry
+
+    lax.fori_loop(0, planes, body, 0)
+
+
+def stencil(src, start, group, coefs, strips, tiles):
+    lane = lax.broadcasted_iota(jnp.int32, (8, LANES), 1)
+    count = src.shape[0]
+    for t in strips:
+        row = HALO + 8 * t
+        planes = [
+            [src[k, start + i, row : row + 8] for k in range(count)] for i in range(group + 2)
+        ]
+        for i in range(group):
+            x = start + i
+            here = planes[i + 1]
+            ahead = [pltpu.roll(value, 1, 1) for value in here]
+            back = [pltpu.roll(value, LANES - 1, 1) for value in here]
+            for k in range(tiles):
+
+                def coef(index):
+                    return coefs[index][x, 8 * t : 8 * t + 8, k * LANES : (k + 1) * LANES]
+
+                total = coef(0) * here[k]
+                total = total + (coef(1) * planes[i][k] + coef(2) * planes[i + 2][k])
+                total = total + (
+                    coef(3) * src[k, x + 1, row - 1 : row + 7]
+                    + coef(4) * src[k, x + 1, row + 1 : row + 9]
+                )
+                left = jnp.where(lane == 0, ahead[k - 1], ahead[k])
+                right = jnp.where(lane == LANES - 1, back[(k + 1) % count], back[k])
+                yield x, t, k, total + (coef(5) * left + coef(6) * right)
 
 
 def transport(planes, q_ref, out_ref, field, middle, coefs, between):
-    height, width = field.shape[1:]
+    tiles = field.shape[0]
     rows, depth = q_ref.shape[1:]
-
-    def first(x, carry):
-        for t, value in enumerate(stencil(field, x, coefs, height, width)):
-            middle[x + 1, 8 * t : 8 * t + 8, :] = value
-        return carry
-
-    def second(x, carry):
-        for t, value in enumerate(stencil(middle, x, coefs, height, width)):
-            part = pl.ds(8 * t, 8)
-            field[x + 1, part, :] = 0.5 * (field[x + 1, part, :] + value)
-        return carry
-
-    def last(x, carry):
-        for t, value in enumerate(stencil(middle, x, coefs, rows, depth)):
-            part = pl.ds(8 * t, 8)
-            out_ref[x, part, :] = 0.5 * (field[x + 1, part, 0:depth] + value)
+    strips = (rows + 2 * HALO) // 8
+    scale = 0.5**STEPS
+
+    group = math.gcd(planes, 4)
+
+    def first(i, carry):
+        for x, t, k, value in stencil(field, group * i, group, coefs, range(strips), tiles):
+            middle[k, x + 1, HALO + 8 * t : HALO + 8 * t + 8] = value
+        return carry
+
+    def second(i, carry):
+        for x, t, k, value in stencil(middle, group * i, group, coefs, range(strips), tiles):
+            part = slice(HALO + 8 * t, HALO + 8 * t + 8)
+            field[k, x + 1, part] = field[k, x + 1, part] + value
+        return carry
+
+    def last(i, carry):
+        inner = range(HALO // 8, strips - HALO // 8)
+        for x, t, k, value in stencil(middle, group * i, group, coefs, inner, depth // LANES):
+            part = slice(HALO + 8 * t, HALO + 8 * t + 8)
+            lanes = slice(k * LANES, (k + 1) * LANES)
+            row = 8 * t - HALO
+            out_ref[x, row : row + 8, lanes] = scale * (field[k, x + 1, part] + value)
         return carry
 
     def step(i, carry):
-        lax.fori_loop(0, planes, first, 0, unroll=4)
-        lax.fori_loop(0, planes, second, 0, unroll=4)
+        lax.fori_loop(0, planes // group, first, 0, unroll=2)
+        lax.fori_loop(0, planes // group, second, 0, unroll=2)
         return carry
 
     lax.fori_loop(0, STEPS - 1, step, 0)
     between()
-    lax.fori_loop(0, planes, first, 0, unroll=4)
-    lax.fori_loop(0, planes, last, 0, unroll=4)
+    lax.fori_loop(0, planes // group, first, 0, unroll=2)
+    lax.fori_loop(0, planes // group, last, 0, unroll=2)
 
 
 def adjoint_kernel(
@@ -199,8 +223,7 @@
     image.clear()
     greet(has, peers)
     mine.start()
-    middle[0] = jnp.zeros(middle.shape[1:], F32)
-    middle[planes + 1] = jnp.zeros(middle.shape[1:], F32)
+    clear_edges(middle)
     expand_kernel(planes, modes_x, modes, v_ref, bx_ref, by_ref, bz_ref, coefs)
     mine.forward()
     image.start()
@@ -223,8 +246,7 @@
     for c in range(3):
         for a in range(modes_x):
             next_ref[c, a] = v_ref[a][:, c * modes : (c + 1) * modes]
-    middle[0] = jnp.zeros(middle.shape[1:], F32)
-    middle[planes + 1] = jnp.zeros(middle.shape[1:], F32)
+    clear_edges(middle)
     gather_field(q_ref, yh_ref, lambda x: zt_ref[x], field)
     expand_kernel(planes, modes_x, modes, v_ref, bx_ref, by_ref, bz_ref, coefs)
     transport(planes, q_ref, out_ref, field, middle, coefs, lambda: None)
@@ -233,18 +255,26 @@
 def project_kernel(
     planes, modes_x, adj_ref, q_ref, yh_ref, zt_ref, bx_ref, by_ref, bz_ref, out_ref, field, forcing, inner
 ):
-    height, width = field.shape[1:]
     rows, depth = q_ref.shape[1:]
+    tiles = field.shape[0]
     gather_field(q_ref, yh_ref, lambda x: zt_ref[x], field)
     by, bz = by_ref[lax.axis_index("ha")], bz_ref.at[lax.axis_index("dev")]
+    start = 2 * HALO
 
     def body(x, carry):
-        plane = field[x + 1]
         half = 0.5 * adj_ref[x]
+
+        def take(plane, offset):
+            part = slice(start + offset, start + offset + rows)
+            parts = [field[k, plane, part] for k in range(depth // LANES)]
+            return jnp.concatenate(parts, axis=1)
+
+        row = jnp.concatenate([field[k, x + 1, start : start + rows] for k in range(tiles)], axis=1)
+        width = tiles * LANES
         slopes = (
-            field[x + 2, 0:rows, 0:depth] - field[x, 0:rows, 0:depth],
-            (pltpu.roll(plane, height - 1, 0) - pltpu.roll(plane, 1, 0))[0:rows, 0:depth],
-            (pltpu.roll(plane, width - 1, 1) - pltpu.roll(plane, 1, 1))[0:rows, 0:depth],
+            take(x + 2, 0) - take(x, 0),
+            take(x + 1, 1) - take(x + 1, -1),
+            (pltpu.roll(row, width - 1, 1) - pltpu.roll(row, 1, 1))[:, 0:depth],
         )
         for c in range(3):
             high, low = split(half * slopes[c])
@@ -253,7 +283,7 @@
             forcing[pl.ds(x * 2 * rows + rows, rows), columns] = low
         return carry
 
-    lax.fori_loop(0, planes, body, 0)
+    lax.fori_loop(0, planes, body, 0, unroll=2)
     chunk = 8
 
     def multiply(i, carry):
@@ -277,11 +307,7 @@
         out_ref[a] = jnp.dot(by, stacked, preferred_element_type=F32)
         return carry
 
-    lax.fori_loop(0, modes_x, finish, 0)
-
-
-def peer_of(index, sides):
-    return {"ha": index // sides, "dev": lax.rem(index, sides)}
+    lax.fori_loop(0, modes_x, finish, 0, unroll=2)
 
 
 MESH = pl.DeviceIdType.MESH
@@ -373,52 +399,69 @@
         return jnp.where(lane < LANES // 2, right_ref[x], left_ref[x])
 
 
-def update_kernel(count, sides, part_ref, old_ref, factor_ref, out_ref, held, send, recv, send2, recv2):
-    me = lax.axis_index("ha") * sides + lax.axis_index("dev")
-    rows = held.shape[1]
+def update_kernel(
+    count_y, count_z, part_ref, old_ref, factor_ref, out_ref, shares, half, held,
+    send_z, recv_z, send_y, recv_y, send_y2, recv_y2, send_z2, recv_z2
+):
+    me_y, me_z = lax.axis_index("ha"), lax.axis_index("dev")
+    large, rows = half.shape[0], held.shape[1]
     barrier = pltpu.get_barrier_semaphore()
-    for d in range(1, count):
-        peer = lax.rem(me + d, count)
-        pl.semaphore_signal(
-            barrier, inc=1, device_id=peer_of(peer, sides), device_id_type=pl.DeviceIdType.MESH
+    peers_y = [lax.rem(me_y + d, count_y) for d in range(1, count_y)]
+    peers_z = [lax.rem(me_z + d, count_z) for d in range(1, count_z)]
+    for axis, peers in (("ha", peers_y), ("dev", peers_z)):
+        for peer in peers:
+            pl.semaphore_signal(barrier, inc=1, device_id={axis: peer}, device_id_type=MESH)
+    pl.semaphore_wait(barrier, count_y + count_z - 2)
+
+    def copy(source, target, send, recv, axis, peer):
+        started = pltpu.make_async_remote_copy(
+            src_ref=source,
+            dst_ref=target,
+            send_sem=send,
+            recv_sem=recv,
+            device_id={axis: peer},
+            device_id_type=MESH,
         )
-    pl.semaphore_wait(barrier, count - 1)
-    mine = pl.ds(pl.multiple_of(me * rows, rows), rows)
-    copies = []
-    for d in range(1, count):
-        peer = lax.rem(me + d, count)
-        copy = pltpu.make_async_remote_copy(
-            src_ref=part_ref.at[pl.ds(pl.multiple_of(peer * rows, rows), rows)],
-            dst_ref=held.at[d],
-            send_sem=send.at[d],
-            recv_sem=recv.at[d],
-            device_id=peer_of(peer, sides),
-            device_id_type=pl.DeviceIdType.MESH,
-        )
-        copy.start()
-        copies.append(copy)
-    total = part_ref[mine]
-    for d in range(1, count):
-        copies[d - 1].wait_recv()
+        started.start()
+        return started
+
+    def span(index, size):
+        return pl.ds(pl.multiple_of(index * size, size), size)
+
+    mine_z = span(me_z, large)
+    mine = pl.ds(pl.multiple_of(me_z * large + me_y * rows, rows), rows)
+    copies = [
+        copy(part_ref.at[span(peer, large)], shares.at[d], send_z.at[d], recv_z.at[d], "dev", peer)
+        for d, peer in enumerate(peers_z)
+    ]
+    total = part_ref[mine_z]
+    for d, started in enumerate(copies):
+        started.wait_recv()
+        total = total + shares[d]
+    half[...] = total
+    copies += [
+        copy(half.at[span(peer, rows)], held.at[d], send_y.at[d], recv_y.at[d], "ha", peer)
+        for d, peer in enumerate(peers_y)
+    ]
+    total = half[span(me_y, rows)]
+    for d, started in enumerate(copies[count_z - 1 :]):
+        started.wait_recv()
         total = total + held[d]
     out_ref[mine] = old_ref[mine] + factor_ref[mine] * total
-    for copy in copies:
-        copy.wait_send()
-    copies = []
-    for d in range(1, count):
-        peer = lax.rem(me + d, count)
-        copy = pltpu.make_async_remote_copy(
-            src_ref=out_ref.at[mine],
-            dst_ref=out_ref.at[mine],
-            send_sem=send2.at[d],
-            recv_sem=recv2.at[d],
-            device_id=peer_of(peer, sides),
-            device_id_type=pl.DeviceIdType.MESH,
-        )
-        copy.start()
-        copies.append(copy)
-    for copy in copies:
-        copy.wait()
+    for started in copies:
+        started.wait_send()
+    copies = [
+        copy(out_ref.at[mine], out_ref.at[mine], send_y2.at[d], recv_y2.at[d], "ha", peer)
+        for d, peer in enumerate(peers_y)
+    ]
+    for started in copies:
+        started.wait()
+    copies = [
+        copy(out_ref.at[mine_z], out_ref.at[mine_z], send_z2.at[d], recv_z2.at[d], "dev", peer)
+        for d, peer in enumerate(peers_z)
+    ]
+    for started in copies:
+        started.wait()
 
 
 VMEM = pl.BlockSpec(memory_space=pltpu.VMEM)
@@ -436,9 +479,10 @@
 
     expand_y, expand_z, project_y, project_z = [], [], [], []
     for i in range(count_y):
-        high, low = halves(basis(wrapped(i * rows, rows, tall, height), height, modes))
+        positions = np.arange(i * rows - HALO, (i + 1) * rows + HALO)
+        high, low = halves(basis(positions, height, modes))
         expand_y.append(np.concatenate([high, high, low], axis=1))
-        high, low = high[:rows].T, low[:rows].T
+        high, low = high[HALO:-HALO].T, low[HALO:-HALO].T
         project_y.append(np.concatenate([high, high, low], axis=1))
     for i in range(count_z):
         high, low = halves(basis(wrapped(i * cols, cols, wide, depth), depth, modes))
@@ -462,7 +506,7 @@
     def widen(value):
         return jnp.pad(value, ((0, 0), (0, 0), (0, LANES - 3 * modes)))
 
-    plane = pltpu.VMEM((planes + 2, tall, wide), F32)
+    plane = pltpu.VMEM((wide // LANES, planes + 2, tall + 2 * HALO, LANES), F32)
     block = jax.ShapeDtypeStruct((planes, rows, cols), F32)
     rims = jax.ShapeDtypeStruct((planes, 2 * HALO, cols), F32)
     sheet = jax.ShapeDtypeStruct((planes, tall, LANES), F32)
@@ -504,15 +548,18 @@
         name="project",
     )
 
-    devices = count_y * count_z
     entries = modes_x * modes
     update = pl.pallas_call(
-        functools.partial(update_kernel, devices, count_z),
+        functools.partial(update_kernel, count_y, count_z),
         out_shape=jax.ShapeDtypeStruct((entries, LANES), F32),
         in_specs=[VMEM, VMEM, VMEM],
         out_specs=VMEM,
-        scratch_shapes=[pltpu.VMEM((devices, entries // devices, LANES), F32)]
-        + [pltpu.SemaphoreType.DMA((devices,))] * 4,
+        scratch_shapes=[
+            pltpu.VMEM((count_z, entries // count_z, LANES), F32),
+            pltpu.VMEM((entries // count_z, LANES), F32),
+            pltpu.VMEM((count_y, entries // count_z // count_y, LANES), F32),
+        ]
+        + [pltpu.SemaphoreType.DMA((n,)) for n in (count_z,) * 2 + (count_y,) * 4 + (count_z,) * 2],
         compiler_params=pltpu.CompilerParams(collective_id=0, has_side_effects=True),
         name="update",
     )

time: 116 us -> 112 us (0.966)
  Pallas kernels: 112 us -> 107 us
    pallas_call x1, Pallas kernels: 12.1 us -> 9.85 us  [per_device(): project(adjoint_end, brain_image, *image_halo, bx, by_back, bz_back)]
where the time goes in v4:
time: 112 us
  Pallas kernels  107 us (96%)
  local copies, waits for them, and re-layouts  3.95 us (4%)
    pallas_call x1, Pallas kernels, per_device(): adjoint_transport(old, bx * -scale, by_wide, bz_wide, adjoint_field, brai...  43.4 us
    pallas_call x1, Pallas kernels, per_device(): image_transport(updated.reshape(modes_x, modes, LANES), bx * scale, by_wi...  32.5 us
    pallas_call x1, Pallas kernels, per_device(): update(partial.reshape(entries, LANES), old.reshape(entries, LANES), factor)  21.6 us
    pallas_call x1, Pallas kernels, per_device(): project(adjoint_end, brain_image, *image_halo, bx, by_back, bz_back)  9.85 us

profile of v4, /device:TPU:0, one launch (start us, length us, event | category | flops | bytes accessed | tf_op | source)
XLA Modules:
  0.0 112.0 jit_solution(12464767390336541227)
XLA Ops:
  0.6 1.7 %copy.13 = f32[16,32,3,32]{3,2,1,0:T(4,128)S(1)} copy(f32[16,32,3,32]{3,1,0,2:T(8,128)} %bitcast.7) | data formatting | bytes 393216 | tf_op jit(solution)/shard_map/transpose | solution.py:567
  2.3 0.4 reshape.18
  2.7 0.7 pad.4.v_ref
  3.4 43.4 %adjoint_transport.1 = (f32[32,32,384]{2,1,0:T(8,128)}, f32[32,16,384]{2,1,0:T(8,128)}, f32[32,48,128]{2,1,0:T(8,128)}) custom-call(f32[16,32,128]{2,1,0:T(8,128)} %pad.4.v_ref, f32[32,16]{1,0:T(8,128)} %constant.28.bx_ref, bf16[8,48,96]{2,1,0:T(8,128)(2,1)} %constant.19.clone.by_ref, bf16[2,128,512]{2,1,0:T(8,128)(2,1)} %constant.21.clone.bz_ref, ...), custom_call_target="tpu_custom_call" | custom-call | tf_op jit(solution)/shard_map/adjoint_transport/pallas_call | solution.py:568
  46.8 9.8 %project.1 = f32[16,32,128]{2,1,0:T(8,128)} custom-call(f32[32,32,384]{2,1,0:T(8,128)} %get-tuple-element.16.adj_ref, f32[32,32,384]{2,1,0:T(8,128)} %q_ref.5, f32[32,16,384]{2,1,0:T(8,128)} %get-tuple-element.9.yh_ref, f32[32,48,128]{2,1,0:T(8,128)} %get-tuple-element.10.zt_ref, f32[32,16]{1,0:T(8,128)} %constant.23.clone.bx_ref, ...), custom_call_target="tpu_custom_call" | custom-call | tf_op jit(solution)/shard_map/project/pallas_call | solution.py:571
  56.7 21.6 %update.1 = f32[512,128]{1,0:T(8,128)} custom-call(f32[512,128]{1,0:T(8,128)} %bitcast.5, f32[512,128]{1,0:T(8,128)} %bitcast.4, f32[512,128]{1,0:T(8,128)} %constant.24.clone.factor_ref), custom_call_target="tpu_custom_call" | custom-call | tf_op jit(solution)/shard_map/update/pallas_call | solution.py:572
  78.3 0.0 copy-start
  78.3 32.5 %image_transport.1 = (f32[32,32,384]{2,1,0:T(8,128)}, f32[3,16,32,32]{3,2,1,0:T(8,128)}) custom-call(f32[16,32,128]{2,1,0:T(8,128)} %bitcast.6, f32[32,16]{1,0:T(8,128)} %constant.29.bx_ref, bf16[8,48,96]{2,1,0:T(8,128)(2,1)} %constant.19.clone.by_ref, bf16[2,128,512]{2,1,0:T(8,128)(2,1)} %constant.21.clone.bz_ref, f32[32,32,384]{2,1,0:T(8,128)} %q_ref.5, ...), custom_call_target="tpu_custom_call" | custom-call | tf_op jit(solution)/shard_map/image_transport/pallas_call | solution.py:573
  110.8 0.0 copy-done
  110.8 1.1 %copy.15 = f32[32,32,384]{2,1,0:T(8,128)} copy(f32[32,32,384]{2,1,0:T(8,128)S(1)} %copy-done) | data formatting | bytes 3145728
Async XLA Ops:
  78.3 32.5 %copy-start = (f32[32,32,384]{2,1,0:T(8,128)S(1)}, f32[32,32,384]{2,1,0:T(8,128)}, u32[]{:S(2)}) copy-start(f32[32,32,384]{2,1,0:T(8,128)} %get-tuple-element.16.adj_ref) | copy-start | bytes 4718596

commit v5 on v4

--- a/solution.py
+++ b/solution.py
@@ -90,7 +90,7 @@
         coefs[0][x] = total
         return carry
 
-    lax.fori_loop(0, planes, body, 0, unroll=2)
+    lax.fori_loop(0, planes, body, 0, unroll=4)
 
 
 def gather_field(q_ref, yh_ref, tile, field):
@@ -211,7 +211,7 @@
 
 def adjoint_kernel(
     planes, modes_x, modes, count_y, count_z, v_ref, bx_ref, by_ref, bz_ref, q_ref, image_ref,
-    out_ref, image_yh, image_zt, yh_ref, left, right, image_left, image_right,
+    out_ref, image_yh, image_zt, old_ref, yh_ref, left, right, image_left, image_right,
     send, recv, image_send, image_recv, field, middle, *coefs
 ):
     has, peers = neighbours(count_y, count_z)
@@ -224,7 +224,10 @@
     greet(has, peers)
     mine.start()
     clear_edges(middle)
-    expand_kernel(planes, modes_x, modes, v_ref, bx_ref, by_ref, bz_ref, coefs)
+    blank = jnp.zeros((modes, LANES - 3 * modes), F32)
+    for a in range(modes_x):
+        old_ref[a] = jnp.concatenate([v_ref[c, a] for c in range(3)] + [blank], axis=1)
+    expand_kernel(planes, modes_x, modes, old_ref, bx_ref, by_ref, bz_ref, coefs)
     mine.forward()
     image.start()
     mine.finish()
@@ -503,9 +506,6 @@
     factor = np.tile(factor, (1, 1, LANES // modes)).astype(np.float32).reshape(-1, LANES)
     scale = 1.0 / math.sqrt(modes_x * modes * modes)
 
-    def widen(value):
-        return jnp.pad(value, ((0, 0), (0, 0), (0, LANES - 3 * modes)))
-
     plane = pltpu.VMEM((wide // LANES, planes + 2, tall + 2 * HALO, LANES), F32)
     block = jax.ShapeDtypeStruct((planes, rows, cols), F32)
     rims = jax.ShapeDtypeStruct((planes, 2 * HALO, cols), F32)
@@ -513,9 +513,11 @@
     work = [plane, plane] + [pltpu.VMEM((planes, tall, wide), F32)] * 7
     adjoint_transport = pl.pallas_call(
         functools.partial(adjoint_kernel, planes, modes_x, modes, count_y, count_z),
-        out_shape=(block, rims, sheet),
+        out_shape=(
+            block, rims, sheet, jax.ShapeDtypeStruct((modes_x, modes, LANES), F32)
+        ),
         in_specs=[VMEM, SMEM, VMEM, VMEM, VMEM, VMEM],
-        out_specs=(VMEM, VMEM, VMEM),
+        out_specs=(VMEM,) * 4,
         scratch_shapes=[pltpu.VMEM(rims.shape, F32)]
         + [pltpu.VMEM(sheet.shape, F32)] * 4
         + [pltpu.SemaphoreType.DMA((6,))] * 4
@@ -564,9 +566,8 @@
         name="update",
     )
 
-    old = widen(velocity_modes.transpose(1, 2, 0, 3).reshape(modes_x, modes, 3 * modes))
-    adjoint_end, *image_halo = adjoint_transport(
-        old, bx * -scale, by_wide, bz_wide, adjoint_field, brain_image
+    adjoint_end, *image_halo, old = adjoint_transport(
+        velocity_modes, bx * -scale, by_wide, bz_wide, adjoint_field, brain_image
     )
     partial = project(adjoint_end, brain_image, *image_halo, bx, by_back, bz_back)
     updated = update(partial.reshape(entries, LANES), old.reshape(entries, LANES), factor)

time: 112 us -> 108 us (0.964)
  local copies, waits for them, and re-layouts: 3.95 us -> 1.15 us
    transpose x1 -> x0, local copies, waits for them, and re-layouts: 1.68 us -> none  [per_device(): velocity_modes.transpose(1, 2, 0, 3).reshape(modes_x, modes, 3 * modes)]
    pallas_call x1, Pallas kernels: 32.5 us -> 31.3 us  [per_device(): image_transport(updated.reshape(modes_x, modes, LANES), bx * scale, by_wi...]
where the time goes in v5:
time: 108 us
  Pallas kernels  106 us (98%)
  local copies, waits for them, and re-layouts  1.15 us (1%)
    pallas_call x1, Pallas kernels, per_device(): adjoint_transport(velocity_modes, bx * -scale, by_wide, bz_wide, adjoint_...  43.6 us
    pallas_call x1, Pallas kernels, per_device(): image_transport(updated.reshape(modes_x, modes, LANES), bx * scale, by_wi...  31.3 us
    pallas_call x1, Pallas kernels, per_device(): update(partial.reshape(entries, LANES), old.reshape(entries, LANES), factor)  21.7 us
    pallas_call x1, Pallas kernels, per_device(): project(adjoint_end, brain_image, *image_halo, bx, by_back, bz_back)  9.85 us

profile of v5, /device:TPU:0, one launch (start us, length us, event | category | flops | bytes accessed | tf_op | source)
XLA Modules:
  0.0 108.2 jit_solution(347019663779961074)
XLA Ops:
  0.6 43.6 %adjoint_transport.1 = (f32[32,32,384]{2,1,0:T(8,128)}, f32[32,16,384]{2,1,0:T(8,128)}, f32[32,48,128]{2,1,0:T(8,128)}, f32[16,32,128]{2,1,0:T(8,128)}) custom-call(f32[3,16,32,32]{3,2,1,0:T(8,128)} %v_ref.1, f32[32,16]{1,0:T(8,128)} %constant.23.bx_ref, bf16[8,48,96]{2,1,0:T(8,128)(2,1)} %constant.16.clone.by_ref, ...), custom_call_target="tpu_custom_call" | custom-call | tf_op jit(solution)/shard_map/adjoint_transport/pallas_call | solution.py:569
  44.2 9.8 %project.1 = f32[16,32,128]{2,1,0:T(8,128)} custom-call(f32[32,32,384]{2,1,0:T(8,128)} %get-tuple-element.18.adj_ref, f32[32,32,384]{2,1,0:T(8,128)} %q_ref.5, f32[32,16,384]{2,1,0:T(8,128)} %get-tuple-element.10.yh_ref, f32[32,48,128]{2,1,0:T(8,128)} %get-tuple-element.11.zt_ref, f32[32,16]{1,0:T(8,128)} %constant.20.clone.bx_ref, ...), custom_call_target="tpu_custom_call" | custom-call | tf_op jit(solution)/shard_map/project/pallas_call | solution.py:572
  54.1 21.7 %update.1 = f32[512,128]{1,0:T(8,128)} custom-call(f32[512,128]{1,0:T(8,128)} %bitcast.3, f32[512,128]{1,0:T(8,128)} %bitcast.5, f32[512,128]{1,0:T(8,128)} %constant.21.clone.factor_ref), custom_call_target="tpu_custom_call" | custom-call | tf_op jit(solution)/shard_map/update/pallas_call | solution.py:573
  75.7 0.0 copy-start
  75.8 31.3 %image_transport.1 = (f32[32,32,384]{2,1,0:T(8,128)}, f32[3,16,32,32]{3,2,1,0:T(8,128)}) custom-call(f32[16,32,128]{2,1,0:T(8,128)} %bitcast.4, f32[32,16]{1,0:T(8,128)} %constant.24.bx_ref, bf16[8,48,96]{2,1,0:T(8,128)(2,1)} %constant.16.clone.by_ref, bf16[2,128,512]{2,1,0:T(8,128)(2,1)} %constant.18.clone.bz_ref, f32[32,32,384]{2,1,0:T(8,128)} %q_ref.5, ...), custom_call_target="tpu_custom_call" | custom-call | tf_op jit(solution)/shard_map/image_transport/pallas_call | solution.py:574
  107.0 0.0 copy-done
  107.0 1.1 %copy.13 = f32[32,32,384]{2,1,0:T(8,128)} copy(f32[32,32,384]{2,1,0:T(8,128)S(1)} %copy-done) | data formatting | bytes 3145728
Async XLA Ops:
  75.7 31.3 %copy-start = (f32[32,32,384]{2,1,0:T(8,128)S(1)}, f32[32,32,384]{2,1,0:T(8,128)}, u32[]{:S(2)}) copy-start(f32[32,32,384]{2,1,0:T(8,128)} %get-tuple-element.18.adj_ref) | copy-start | bytes 4718596
